TPU v7x, 32 devices: a whole 2x2x4 slice. The times are simulated.
32 devices in a mesh: dp: 8 (over z, x), tensor: 4 (over y, core).
Axes of the slice: x: 2, y: 2, z: 4, core: 2. Of those that a mesh axis runs over, the one named last changes fastest.
Arguments:
- tokens: bfloat16 [8, 1024, 1152], P('dp', 'tensor'), may hold values from -6 to 6
- conditioning: float32 [8, 1152], P('dp', 'tensor'), may hold values from -6 to 6
- out_grad: bfloat16 [8, 1024, 1152], P('dp', 'tensor'), may hold values from -6 to 6
- qkv_weight: float32 [3, 1152, 1152], P(None, 'dp', 'tensor'), may hold values from -0.1875 to 0.1875
- out_weight: float32 [1152, 1152], P('dp', 'tensor'), may hold values from -0.75 to 0.75
- up_weight: float32 [1152, 4608], P('dp', 'tensor'), may hold values from -0.1875 to 0.1875
- down_weight: float32 [1152, 4608], P('dp', 'tensor'), may hold values from -0.09375 to 0.09375
- ada_weight: float32 [6, 1152, 1152], P(None, 'dp', 'tensor'), may hold values from -0.1875 to 0.1875
- qkv_moment: float32 [3, 1152, 1152], P(None, 'dp', 'tensor'), may hold values from -0.00030517578 to 0.00030517578
- out_moment: float32 [1152, 1152], P('dp', 'tensor'), may hold values from -0.00030517578 to 0.00030517578
- up_moment: float32 [1152, 4608], P('dp', 'tensor'), may hold values from -0.00030517578 to 0.00030517578
- down_moment: float32 [1152, 4608], P('dp', 'tensor'), may hold values from -0.00030517578 to 0.00030517578
- ada_moment: float32 [6, 1152, 1152], P(None, 'dp', 'tensor'), may hold values from -0.00030517578 to 0.00030517578
- qkv_square: float32 [3, 1152, 1152], P(None, 'dp', 'tensor'), may hold values from 4.1862246e-11 to 1.6744899e-10
- out_square: float32 [1152, 1152], P('dp', 'tensor'), may hold values from 4.1862246e-11 to 1.6744899e-10
- up_square: float32 [1152, 4608], P('dp', 'tensor'), may hold values from 4.1862246e-11 to 1.6744899e-10
- down_square: float32 [1152, 4608], P('dp', 'tensor'), may hold values from 4.1862246e-11 to 1.6744899e-10
- ada_square: float32 [6, 1152, 1152], P(None, 'dp', 'tensor'), may hold values from 4.1862246e-11 to 1.6744899e-10
Outputs:
- block_out: bfloat16 [8, 1024, 1152], P('dp', 'tensor')
- input_grad: float32 [8, 1024, 1152], P('dp', 'tensor')
- cond_grad: float32 [8, 1152], P('dp', 'tensor')
- grad_norm: float32 [], replicated
- qkv_new: float32 [3, 1152, 1152], P(None, 'dp', 'tensor')
- out_new: float32 [1152, 1152], P('dp', 'tensor')
- up_new: float32 [1152, 4608], P('dp', 'tensor')
- down_new: float32 [1152, 4608], P('dp', 'tensor')
- ada_new: float32 [6, 1152, 1152], P(None, 'dp', 'tensor')
- qkv_moment_new: float32 [3, 1152, 1152], P(None, 'dp', 'tensor')
- out_moment_new: float32 [1152, 1152], P('dp', 'tensor')
- up_moment_new: float32 [1152, 4608], P('dp', 'tensor')
- down_moment_new: float32 [1152, 4608], P('dp', 'tensor')
- ada_moment_new: float32 [6, 1152, 1152], P(None, 'dp', 'tensor')
- qkv_square_new: float32 [3, 1152, 1152], P(None, 'dp', 'tensor')
- out_square_new: float32 [1152, 1152], P('dp', 'tensor')
- up_square_new: float32 [1152, 4608], P('dp', 'tensor')
- down_square_new: float32 [1152, 4608], P('dp', 'tensor')
- ada_square_new: float32 [6, 1152, 1152], P(None, 'dp', 'tensor')
All inputs are finite; a program needn't handle non-finite values.
Results may differ from a plain program's by a relative error of at most 0.017.
The roundings to bfloat16 on the way count: a program that leaves them out, or rounds other values in their place, can miss the bound.
Values may be sent and summed in bfloat16 or wider, within the bound.
No kernel may reach another device: no remote copies, remote signals or barrier semaphores. Data moves between devices by JAX's collectives and lax.ppermute only.
A program may use at most 192 MiB of HBM per device.

v0:
```python
import jax
import jax.numpy as jnp
from jax import lax
from jax.sharding import PartitionSpec as P

HEAD_DIM = 72
STEP = 10


EPS_NORM = 1e-06
CLIP_NORM = 1.0
LEARN_RATE = 0.05
WEIGHT_DECAY = 0.1
BETA_ONE = 0.9
BETA_TWO = 0.999
EPS_ADAM = 1e-08


def layer_norm(values):
    centre = values - jnp.mean(values, axis=-1, keepdims=True)
    spread = jnp.mean(centre * centre, axis=-1, keepdims=True)
    return centre * lax.rsqrt(spread + EPS_NORM)


def modulate(values, shift_row, scale_row):
    return layer_norm(values) * (1.0 + scale_row[:, None, :]) + shift_row[:, None, :]


def gelu_tanh(values):
    return jax.nn.gelu(values, approximate=True)


def to_blocks(stacked, block_rows):
    leading, positions = (stacked.shape[0], stacked.shape[1])
    shaped = stacked.reshape((leading, positions // block_rows, block_rows) + stacked.shape[2:])
    return jnp.moveaxis(shaped, 1, 0)


def from_blocks(stacked):
    swapped = jnp.moveaxis(stacked, 0, 1)
    return swapped.reshape(
        (swapped.shape[0], swapped.shape[1] * swapped.shape[2]) + swapped.shape[3:]
    )


def adam_update(weight, gradient, moment, square, clip_factor):
    clipped = gradient * clip_factor
    moment_new = BETA_ONE * moment + (1.0 - BETA_ONE) * clipped
    square_new = BETA_TWO * square + (1.0 - BETA_TWO) * clipped * clipped
    mean_hat = moment_new / (1.0 - BETA_ONE**STEP)
    square_hat = square_new / (1.0 - BETA_TWO**STEP)
    weight_new = weight - LEARN_RATE * (
        mean_hat / (jnp.sqrt(square_hat) + EPS_ADAM) + WEIGHT_DECAY * weight
    )
    return (weight_new, moment_new, square_new)


def on_device(
    tokens,
    conditioning,
    out_grad,
    qkv_weight,
    out_weight,
    up_weight,
    down_weight,
    ada_weight,
    qkv_moment,
    out_moment,
    up_moment,
    down_moment,
    ada_moment,
    qkv_square,
    out_square,
    up_square,
    down_square,
    ada_square,
):
    low_qkv = qkv_weight.astype(jnp.bfloat16)
    low_out = out_weight.astype(jnp.bfloat16)[None]
    low_up = up_weight.astype(jnp.bfloat16)[None]
    low_down = down_weight.astype(jnp.bfloat16)[None]
    low_ada = ada_weight.astype(jnp.bfloat16)
    full_qkv, full_out, full_up, full_down, full_ada = (
        lax.all_gather(low_qkv, "dp", axis=1, tiled=True),
        lax.all_gather(low_out, "dp", axis=1, tiled=True),
        lax.all_gather(low_up, "dp", axis=1, tiled=True),
        lax.all_gather(low_down, "dp", axis=1, tiled=True),
        lax.all_gather(low_ada, "dp", axis=1, tiled=True),
    )
    full_out, full_up, full_down = (full_out[0], full_up[0], full_down[0])
    signal, silu_back = jax.vjp(jax.nn.silu, conditioning)
    signal_low = signal.astype(jnp.bfloat16)
    mod_terms = jnp.einsum("bi,kni->bkn", signal_low, full_ada, preferred_element_type=jnp.float32)
    modulation = lax.psum(mod_terms, "tensor")
    shift_one, scale_one, gate_one = (modulation[:, 0], modulation[:, 1], modulation[:, 2])
    shift_two, scale_two, gate_two = (modulation[:, 3], modulation[:, 4], modulation[:, 5])
    residual = tokens.astype(jnp.float32)
    normed_one, norm_one_back = jax.vjp(modulate, residual, shift_one, scale_one)
    seq_one = lax.all_gather(normed_one.astype(jnp.bfloat16), "tensor", axis=1, tiled=True)
    latents_here, length, model_width = seq_one.shape
    projected = jnp.einsum(
        "bsd,tde->tbse", seq_one, full_qkv, preferred_element_type=jnp.float32
    ).astype(jnp.bfloat16)
    local_width = projected.shape[-1]
    heads_here = local_width // HEAD_DIM
    heads_split = projected.reshape(3, latents_here, length, heads_here, HEAD_DIM)
    queries, key_rows, values = (heads_split[0], heads_split[1], heads_split[2])
    block_rows = min(512, length)
    score_scale = HEAD_DIM ** (-0.5)

    def forward_block(query_part):
        scores = (
            jnp.einsum("bqhe,bkhe->bhqk", query_part, key_rows, preferred_element_type=jnp.float32)
            * score_scale
        )
        row_peak = jnp.max(scores, axis=-1, keepdims=True)
        exponent = jnp.exp(scores - row_peak)
        row_total = jnp.sum(exponent, axis=-1, keepdims=True)
        probability = (exponent / row_total).astype(jnp.bfloat16)
        mixture = jnp.einsum(
            "bhqk,bkhe->bqhe", probability, values, preferred_element_type=jnp.float32
        )
        return (mixture, (row_peak + jnp.log(row_total))[..., 0])

    mixed_blocks, log_totals = lax.map(forward_block, to_blocks(queries, block_rows))
    attended = (
        from_blocks(mixed_blocks).reshape(latents_here, length, local_width).astype(jnp.bfloat16)
    )
    attn_terms = jnp.einsum("bse,de->bsd", attended, full_out, preferred_element_type=jnp.float32)
    attn_rows = lax.psum_scatter(attn_terms, "tensor", scatter_dimension=1, tiled=True)
    middle = residual + gate_one[:, None, :] * attn_rows
    normed_two, norm_two_back = jax.vjp(modulate, middle, shift_two, scale_two)
    seq_two = lax.all_gather(normed_two.astype(jnp.bfloat16), "tensor", axis=1, tiled=True)
    pre_act = jnp.einsum("bsd,df->bsf", seq_two, full_up, preferred_element_type=jnp.float32)
    activated, gelu_back = jax.vjp(gelu_tanh, pre_act)
    hidden = activated.astype(jnp.bfloat16)
    mlp_terms = jnp.einsum("bsf,df->bsd", hidden, full_down, preferred_element_type=jnp.float32)
    mlp_rows = lax.psum_scatter(
        mlp_terms.astype(jnp.bfloat16), "tensor", scatter_dimension=1, tiled=True
    ).astype(jnp.float32)
    block_out = (middle + gate_two[:, None, :] * mlp_rows).astype(jnp.bfloat16)
    back_qkv, back_out, back_up, back_down, back_ada = (
        full_qkv,
        full_out,
        full_up,
        full_down,
        full_ada,
    )
    grad_final = out_grad.astype(jnp.float32)
    grad_gate_two = jnp.sum(grad_final * mlp_rows, axis=1)
    grad_mlp = (grad_final * gate_two[:, None, :]).astype(jnp.bfloat16)
    grad_mlp_seq = lax.all_gather(grad_mlp, "tensor", axis=1, tiled=True)
    grad_down = jnp.einsum("bsd,bsf->df", grad_mlp_seq, hidden, preferred_element_type=jnp.float32)
    grad_hidden = jnp.einsum(
        "bsd,df->bsf", grad_mlp_seq, back_down, preferred_element_type=jnp.float32
    )
    grad_pre = gelu_back(grad_hidden)[0].astype(jnp.bfloat16)
    grad_up = jnp.einsum("bsd,bsf->df", seq_two, grad_pre, preferred_element_type=jnp.float32)
    grad_two_terms = jnp.einsum(
        "bsf,df->bsd", grad_pre, back_up, preferred_element_type=jnp.float32
    )
    grad_normed_two = lax.psum_scatter(grad_two_terms, "tensor", scatter_dimension=1, tiled=True)
    grad_mid_norm, grad_shift_two, grad_scale_two = norm_two_back(grad_normed_two)
    grad_middle = grad_final + grad_mid_norm
    grad_gate_one = jnp.sum(grad_middle * attn_rows, axis=1)
    grad_attn = (grad_middle * gate_one[:, None, :]).astype(jnp.bfloat16)
    grad_attn_seq = lax.all_gather(grad_attn, "tensor", axis=1, tiled=True)
    grad_out = jnp.einsum(
        "bsd,bse->de", grad_attn_seq, attended, preferred_element_type=jnp.float32
    )
    grad_attended = jnp.einsum(
        "bsd,de->bse", grad_attn_seq, back_out, preferred_element_type=jnp.float32
    )
    grad_attended = grad_attended.astype(jnp.bfloat16).reshape(
        latents_here, length, heads_here, HEAD_DIM
    )

    def backward_block(carried, sample):
        grad_keys, grad_values = carried
        query_part, grad_part, log_part = sample
        scores = (
            jnp.einsum("bqhe,bkhe->bhqk", query_part, key_rows, preferred_element_type=jnp.float32)
            * score_scale
        )
        probability = jnp.exp(scores - log_part[..., None])
        grad_probability = jnp.einsum(
            "bqhe,bkhe->bhqk", grad_part, values, preferred_element_type=jnp.float32
        )
        row_inner = jnp.sum(probability * grad_probability, axis=-1, keepdims=True)
        grad_scores = (probability * (grad_probability - row_inner)).astype(jnp.bfloat16)
        grad_query = (
            jnp.einsum("bhqk,bkhe->bqhe", grad_scores, key_rows, preferred_element_type=jnp.float32)
            * score_scale
        )
        grad_keys = (
            grad_keys
            + jnp.einsum(
                "bhqk,bqhe->bkhe", grad_scores, query_part, preferred_element_type=jnp.float32
            )
            * score_scale
        )
        grad_values = grad_values + jnp.einsum(
            "bhqk,bqhe->bkhe",
            probability.astype(jnp.bfloat16),
            grad_part,
            preferred_element_type=jnp.float32,
        )
        return ((grad_keys, grad_values), grad_query)

    zero_grad = jnp.zeros(key_rows.shape, jnp.float32)
    (grad_keys, grad_values), grad_blocks = lax.scan(
        backward_block,
        (zero_grad, zero_grad),
        (to_blocks(queries, block_rows), to_blocks(grad_attended, block_rows), log_totals),
    )
    grad_queries = from_blocks(grad_blocks)
    grad_projected = (
        jnp.stack([grad_queries, grad_keys, grad_values])
        .reshape(3, latents_here, length, local_width)
        .astype(jnp.bfloat16)
    )
    grad_qkv = jnp.einsum(
        "tbse,bsd->tde", grad_projected, seq_one, preferred_element_type=jnp.float32
    )
    grad_one_terms = jnp.einsum(
        "tbse,tde->bsd", grad_projected, back_qkv, preferred_element_type=jnp.float32
    )
    grad_normed_one = lax.psum_scatter(grad_one_terms, "tensor", scatter_dimension=1, tiled=True)
    grad_in_norm, grad_shift_one, grad_scale_one = norm_one_back(grad_normed_one)
    input_grad = grad_middle + grad_in_norm
    grad_mod_local = jnp.stack(
        [
            grad_shift_one,
            grad_scale_one,
            grad_gate_one,
            grad_shift_two,
            grad_scale_two,
            grad_gate_two,
        ],
        axis=1,
    )
    grad_modulation = lax.psum(grad_mod_local, "tensor").astype(jnp.bfloat16)
    grad_ada = jnp.einsum(
        "bkn,bi->kni", grad_modulation, signal_low, preferred_element_type=jnp.float32
    )
    grad_signal = jnp.einsum(
        "bkn,kni->bi", grad_modulation, back_ada, preferred_element_type=jnp.float32
    )
    cond_grad = silu_back(grad_signal)[0]
    summed_qkv, summed_out, summed_up, summed_down, summed_ada = (
        lax.psum_scatter(grad_qkv, "dp", scatter_dimension=1, tiled=True),
        lax.psum_scatter(grad_out[None], "dp", scatter_dimension=1, tiled=True),
        lax.psum_scatter(grad_up[None], "dp", scatter_dimension=1, tiled=True),
        lax.psum_scatter(grad_down[None], "dp", scatter_dimension=1, tiled=True),
        lax.psum_scatter(grad_ada, "dp", scatter_dimension=1, tiled=True),
    )
    summed_out, summed_up, summed_down = (summed_out[0], summed_up[0], summed_down[0])
    local_squares = jnp.sum(summed_qkv * summed_qkv) + jnp.sum(summed_out * summed_out)
    local_squares = (
        local_squares + jnp.sum(summed_up * summed_up) + jnp.sum(summed_down * summed_down)
    )
    local_squares = local_squares + jnp.sum(summed_ada * summed_ada)
    total_squares = lax.psum(local_squares, ("dp", "tensor"))
    grad_norm = jnp.sqrt(total_squares)
    clip_factor = CLIP_NORM / jnp.maximum(grad_norm, CLIP_NORM)
    qkv_new, qkv_moment_new, qkv_square_new = adam_update(
        qkv_weight, summed_qkv, qkv_moment, qkv_square, clip_factor
    )
    out_new, out_moment_new, out_square_new = adam_update(
        out_weight, summed_out, out_moment, out_square, clip_factor
    )
    up_new, up_moment_new, up_square_new = adam_update(
        up_weight, summed_up, up_moment, up_square, clip_factor
    )
    down_new, down_moment_new, down_square_new = adam_update(
        down_weight, summed_down, down_moment, down_square, clip_factor
    )
    ada_new, ada_moment_new, ada_square_new = adam_update(
        ada_weight, summed_ada, ada_moment, ada_square, clip_factor
    )
    return (
        block_out,
        input_grad,
        cond_grad,
        grad_norm,
        qkv_new,
        out_new,
        up_new,
        down_new,
        ada_new,
        qkv_moment_new,
        out_moment_new,
        up_moment_new,
        down_moment_new,
        ada_moment_new,
        qkv_square_new,
        out_square_new,
        up_square_new,
        down_square_new,
        ada_square_new,
    )


def solution(mesh):
    placed = (
        P("dp", "tensor", None),
        P("dp", "tensor"),
        P("dp", "tensor", None),
        P(None, "dp", "tensor"),
        P("dp", "tensor"),
        P("dp", "tensor"),
        P("dp", "tensor"),
        P(None, "dp", "tensor"),
        P(None, "dp", "tensor"),
        P("dp", "tensor"),
        P("dp", "tensor"),
        P("dp", "tensor"),
        P(None, "dp", "tensor"),
        P(None, "dp", "tensor"),
        P("dp", "tensor"),
        P("dp", "tensor"),
        P("dp", "tensor"),
        P(None, "dp", "tensor"),
    )
    return jax.shard_map(
        on_device,
        mesh=mesh,
        in_specs=placed,
        out_specs=(
            P("dp", "tensor", None),
            P("dp", "tensor", None),
            P("dp", "tensor"),
            P(),
            P(None, "dp", "tensor"),
            P("dp", "tensor"),
            P("dp", "tensor"),
            P("dp", "tensor"),
            P(None, "dp", "tensor"),
            P(None, "dp", "tensor"),
            P("dp", "tensor"),
            P("dp", "tensor"),
            P("dp", "tensor"),
            P(None, "dp", "tensor"),
            P(None, "dp", "tensor"),
            P("dp", "tensor"),
            P("dp", "tensor"),
            P("dp", "tensor"),
            P(None, "dp", "tensor"),
        ),
        check_vma=False,
    )
```

profile of v0, /device:TPU:0, one launch (start us, length us, event | category | flops | bytes accessed | tf_op | source)
XLA Modules:
  0.0 1298.0 jit_solution(15768447687266753402)
XLA Ops:
  11.0 89.6 %all-gather.12.cloned.1.call-done = bf16[6,1152,288]{2,1,0:T(8,128)(2,1)} async-done(((bf16[6,144,288]{2,1,0:T(8,128)(2,1)}), bf16[6,1152,288]{2,1,0:T(8,128)(2,1)}) %all-gather.12.cloned.1.call-update) | async-done | bytes 3981328 | tf_op jit(solution)/shard_map/all_gather | solution.py:88
  104.7 10.9 psum.21
  116.9 36.7 %all-gather = bf16[1152,288]{1,0:T(8,128)(2,1)} all-gather(bf16[144,288]{1,0:T(8,128)(2,1)S(1)} %convert_element_type.114), channel_id=2, replica_groups=mesh['dp'=8,'tensor'=4] {'dp'}, dimensions={0}, use_global_device_ids=true | all-gather | bytes 746496 | tf_op jit(solution)/shard_map/all_gather | solution.py:85
  153.7 11.9 all-gather.16.cloned.1.call-done
  165.6 26.3 %all-gather.14.cloned.1.call-done = bf16[1,1024,1152]{2,1,0:T(8,128)(2,1)} async-done(((bf16[1,256,1152]{2,1,0:T(8,128)(2,1)}), bf16[1,1024,1152]{2,1,0:T(8,128)(2,1)}) %all-gather.14.cloned.1.call-update) | async-done | bytes 2359312 | tf_op jit(solution)/shard_map/all_gather | solution.py:99
  197.5 10.8 while.27
  215.5 46.1 %reduce-scatter.11.cloned.1.call-done = f32[1,256,1152]{2,1,0:T(8,128)} async-done(((f32[1,1024,1152]{2,1,0:T(8,128)}), f32[1,256,1152]{2,1,0:T(8,128)}) %reduce-scatter.11.cloned.1.call-update) | async-done | bytes 1179664 | tf_op jit(solution)/shard_map/reduce_scatter | solution.py:130
  268.0 51.5 %all-gather.24.cloned.1.call-done = bf16[1152,1152]{1,0:T(8,128)(2,1)} async-done(((bf16[144,1152]{1,0:T(8,128)(2,1)}), bf16[1152,1152]{1,0:T(8,128)(2,1)}) %all-gather.24.cloned.1.call-update) | async-done | bytes 2654224 | tf_op jit(solution)/shard_map/all_gather | solution.py:86
  319.5 24.8 %all-gather.18.cloned.1.call-done = bf16[1,1024,1152]{2,1,0:T(8,128)(2,1)} async-done(((bf16[1,256,1152]{2,1,0:T(8,128)(2,1)}), bf16[1,1024,1152]{2,1,0:T(8,128)(2,1)}) %all-gather.18.cloned.1.call-update) | async-done | bytes 2359312 | tf_op jit(solution)/shard_map/all_gather | solution.py:133
  352.4 49.9 %all-gather.26.cloned.1.call-done = bf16[1152,1152]{1,0:T(8,128)(2,1)} async-done(((bf16[144,1152]{1,0:T(8,128)(2,1)}), bf16[1152,1152]{1,0:T(8,128)(2,1)}) %all-gather.26.cloned.1.call-update) | async-done | bytes 2654224 | tf_op jit(solution)/shard_map/all_gather | solution.py:87
  402.3 24.9 %all-gather.20.cloned.1.call-done = bf16[1,1024,1152]{2,1,0:T(8,128)(2,1)} async-done(((bf16[1,256,1152]{2,1,0:T(8,128)(2,1)}), bf16[1,1024,1152]{2,1,0:T(8,128)(2,1)}) %all-gather.20.cloned.1.call-update) | async-done | bytes 2359312 | tf_op jit(solution)/shard_map/all_gather | solution.py:152
  427.2 9.1 fusion.50
  451.9 38.9 %reduce-scatter.15.cloned.1.call-done = f32[1,256,1152]{2,1,0:T(8,128)} async-done(((f32[1,1024,1152]{2,1,0:T(8,128)}), f32[1,256,1152]{2,1,0:T(8,128)}) %reduce-scatter.15.cloned.1.call-update) | async-done | bytes 1179664 | tf_op jit(solution)/shard_map/reduce_scatter | solution.py:162
  493.1 33.2 %reduce-scatter.13.cloned.1.call-done = bf16[1,256,1152]{2,1,0:T(8,128)(2,1)} async-done(((bf16[1,1024,1152]{2,1,0:T(8,128)(2,1)}), bf16[1,256,1152]{2,1,0:T(8,128)(2,1)}) %reduce-scatter.13.cloned.1.call-update) | async-done | bytes 589840 | tf_op jit(solution)/shard_map/reduce_scatter | solution.py:138
  531.4 24.0 %all-gather.22.cloned.1.call-done = bf16[1,1024,1152]{2,1,0:T(8,128)(2,1)} async-done(((bf16[1,256,1152]{2,1,0:T(8,128)(2,1)}), bf16[1,1024,1152]{2,1,0:T(8,128)(2,1)}) %all-gather.22.cloned.1.call-update) | async-done | bytes 2359312 | tf_op jit(solution)/shard_map/all_gather | solution.py:167
  564.6 22.2 %while.28 = (s32[]{:T(128)}, f32[1,1024,4,72]{1,3,2,0:T(8,128)S(1)}, f32[1,1024,4,72]{1,3,2,0:T(8,128)S(1)}, bf16[2,1,512,4,72]{2,4,3,1,0:T(8,128)(2,1)}, bf16[2...) while((s32[]{:T(128)}, ...), condition=%wide.region_16.17_spmd.clone, body=%wide.region_14.16_spmd.clone.sunk | while | flops 1536735232 | bytes 80666888 | solution.py:211
  637.7 9.0 reshape.443
  658.2 11.7 psum.22
  677.0 75.3 %reduce-scatter.21.cloned.1.call-done = f32[1,144,1152]{2,1,0:T(8,128)} async-done(((f32[1,1152,1152]{2,1,0:T(8,128)}), f32[1,144,1152]{2,1,0:T(8,128)}) %reduce-scatter.21.cloned.1.call-update) | async-done | bytes 663568 | tf_op jit(solution)/shard_map/reduce_scatter | solution.py:254
  754.2 106.0 %reduce-scatter.19.cloned.1.call-done = f32[1,144,1152]{2,1,0:T(8,128)} async-done(((f32[1,1152,1152]{2,1,0:T(8,128)}), f32[1,144,1152]{2,1,0:T(8,128)}) %reduce-scatter.19.cloned.1.call-update) | async-done | bytes 663568 | tf_op jit(solution)/shard_map/reduce_scatter | solution.py:253
  862.0 95.0 %all-reduce.3.cloned.1.call-done = f32[1,1152,288]{2,0,1:T(1,128)} async-done(((f32[1,1152,288]{2,0,1:T(1,128)}), f32[1,1152,288]{2,0,1:T(1,128)}) %all-reduce.3.cloned.1.call-update) | async-done | bytes 1327120
  959.0 88.9 %reduce-scatter.25.cloned.1.call-done = f32[144,864]{1,0:T(8,128)} async-done(((f32[1152,864]{1,0:T(8,128)}), f32[144,864]{1,0:T(8,128)}) %reduce-scatter.25.cloned.1.call-update) | async-done | bytes 497680
  1053.3 177.6 %reduce-scatter.23.cloned.1.call-done = f32[6,144,288]{2,1,0:T(8,128)} async-done(((f32[6,1152,288]{2,1,0:T(8,128)}), f32[6,144,288]{2,1,0:T(8,128)}) %reduce-scatter.23.cloned.1.call-update) | async-done | bytes 995344 | tf_op jit(solution)/shard_map/reduce_scatter | solution.py:255
  1237.9 39.3 %psum.23 = f32[]{:T(128)} all-reduce(f32[]{:T(128)S(6)} %add.225), channel_id=1, replica_groups=mesh['dp'=8,'tensor'=4] {'dp','tensor'}, use_global_device_ids=true, to_apply=%region_37.38 | all-reduce | flops 1 | bytes 8 | tf_op jit(solution)/shard_map/psum | solution.py:263
  (262 shorter events, 196.3 us)
Async XLA Ops:
  7.2 93.5 %copy-start.47 = (f32[1,288]{1,0:T(1,128)S(1)}, f32[1,288]{1,0:T(1,128)}, u32[]{:S(2)}) copy-start(f32[1,288]{1,0:T(1,128)} %param.23) | copy-start | bytes 3460
  7.2 93.5 %all-gather.12.cloned.1.call-start = ((), (), s32[]{:S(2)}) async-start(), calls=%async_computation.8 | async-start | bytes 5971968 | tf_op jit(solution)/shard_map/all_gather | solution.py:88
  9.6 156.0 %all-gather.16.cloned.1.call-start = ((), (), s32[]{:S(2)}) async-start(), calls=%async_computation.10 | async-start | bytes 2985984 | tf_op jit(solution)/shard_map/all_gather | solution.py:84
  10.5 181.4 %all-gather.14.cloned.1.call-start = ((), (), s32[]{:S(2)}) async-start(), calls=%async_computation.9 | async-start | bytes 2949120 | tf_op jit(solution)/shard_map/all_gather | solution.py:99
  10.7 105.0 %copy-start.43 = (f32[256]{0:T(256)}, f32[256]{0:T(256)S(1)}, u32[]{:S(2)}) copy-start(f32[256]{0:T(256)S(1)} %broadcast_multiply_fusion.2) | copy-start | bytes 3076
  11.0 93.7 %copy-start.50 = (f32[256]{0:T(256)}, f32[256]{0:T(256)S(1)}, u32[]{:S(2)}) copy-start(f32[256]{0:T(256)S(1)} %fusion.83) | copy-start | bytes 3076
  11.0 104.7 %copy-start.45 = (f32[256]{0:T(256)}, f32[256]{0:T(256)S(1)}, u32[]{:S(2)}) copy-start(f32[256]{0:T(256)S(1)} %fusion.104) | copy-start | bytes 3076
  11.0 105.9 %copy-start.25 = (f32[144,288]{1,0:T(8,128)S(1)}, f32[144,288]{1,0:T(8,128)}, u32[]{:S(2)}) copy-start(f32[144,288]{1,0:T(8,128)} %param.26) | copy-start | bytes 497668
  116.8 144.8 %reduce-scatter.11.cloned.1.call-start = ((), (), s32[]{:S(2)}) async-start(), calls=%async_computation.11 | async-start | bytes 5898240 | tf_op jit(solution)/shard_map/reduce_scatter | solution.py:130
  213.6 105.9 %all-gather.24.cloned.1.call-start = ((), (), s32[]{:S(2)}) async-start(), calls=%async_computation.21 | async-start | bytes 2985984 | tf_op jit(solution)/shard_map/all_gather | solution.py:86
  215.5 128.8 %all-gather.18.cloned.1.call-start = ((), (), s32[]{:S(2)}) async-start(), calls=%async_computation.12 | async-start | bytes 2949120 | tf_op jit(solution)/shard_map/all_gather | solution.py:133
  264.5 137.7 %all-gather.26.cloned.1.call-start = ((), (), s32[]{:S(2)}) async-start(), calls=%async_computation.22 | async-start | bytes 2985984 | tf_op jit(solution)/shard_map/all_gather | solution.py:87
  266.9 160.3 %all-gather.20.cloned.1.call-start = ((), (), s32[]{:S(2)}) async-start(), calls=%async_computation.14 | async-start | bytes 2949120 | tf_op jit(solution)/shard_map/all_gather | solution.py:152
  267.9 222.9 %reduce-scatter.15.cloned.1.call-start = ((), (), s32[]{:S(2)}) async-start(), calls=%async_computation.15 | async-start | bytes 5898240 | tf_op jit(solution)/shard_map/reduce_scatter | solution.py:162
  442.9 83.5 %reduce-scatter.13.cloned.1.call-start = ((), (), s32[]{:S(2)}) async-start(), calls=%async_computation.13 | async-start | bytes 2949120 | tf_op jit(solution)/shard_map/reduce_scatter | solution.py:138
  451.9 103.4 %all-gather.22.cloned.1.call-start = ((), (), s32[]{:S(2)}) async-start(), calls=%async_computation.16 | async-start | bytes 2949120 | tf_op jit(solution)/shard_map/all_gather | solution.py:167
  531.1 120.1 %reduce-scatter.17.cloned.1.call-start = ((), (), s32[]{:S(2)}) async-start(), calls=%async_computation.17 | async-start | bytes 5898240 | tf_op jit(solution)/shard_map/reduce_scatter | solution.py:228
  596.5 155.8 %reduce-scatter.21.cloned.1.call-start = ((), (), s32[]{:S(2)}) async-start(), calls=%async_computation.19 | async-start | bytes 5971968 | tf_op jit(solution)/shard_map/reduce_scatter | solution.py:254
  606.9 253.3 %reduce-scatter.19.cloned.1.call-start = ((), (), s32[]{:S(2)}) async-start(), calls=%async_computation.18 | async-start | bytes 5971968 | tf_op jit(solution)/shard_map/reduce_scatter | solution.py:253
  615.9 341.0 %all-reduce.3.cloned.1.call-start = ((), (), s32[]{:S(2)}) async-start(), calls=%async_computation.24 | async-start | bytes 3538944
  623.1 424.8 %reduce-scatter.25.cloned.1.call-start = ((), (), s32[]{:S(2)}) async-start(), calls=%async_computation.23 | async-start | bytes 4644864
  646.8 584.1 %reduce-scatter.23.cloned.1.call-start = ((), (), s32[]{:S(2)}) async-start(), calls=%async_computation.20 | async-start | bytes 11943936 | tf_op jit(solution)/shard_map/reduce_scatter | solution.py:255
  959.0 274.9 %copy-start.48 = (f32[1,288]{1,0:T(1,128)S(1)}, f32[1,288]{1,0:T(1,128)}, u32[]{:S(2)}) copy-start(f32[1,288]{1,0:T(1,128)} %param.23) | copy-start | bytes 3460
  1233.9 47.5 %copy-start.26 = (f32[144,288]{1,0:T(8,128)S(1)}, f32[144,288]{1,0:T(8,128)}, u32[]{:S(2)}) copy-start(f32[144,288]{1,0:T(8,128)} %param.26) | copy-start | bytes 497668
  (54 other events, 347.7 us)
Sparse Core Ops, SparseCore 0:
  10.9 89.7 all-gather.11
  103.5 62.0 all-gather.15
  167.7 24.1 all-gather.13
  213.8 47.8 reduce-scatter.10
  264.4 55.0 all-gather.23
  321.6 22.6 all-gather.17
  347.2 55.0 all-gather.25
  404.5 22.6 all-gather.19
  443.0 47.8 reduce-scatter.14
  493.2 33.0 reduce-scatter.12
  531.2 24.0 all-gather.21
  596.6 47.8 reduce-scatter.16
  648.1 104.1 reduce-scatter.20
  756.2 103.9 reduce-scatter.18
  863.6 93.3 all-reduce.2
  960.8 87.0 reduce-scatter.24
  1051.3 179.5 reduce-scatter.22
where the time goes:
time: 1310 us; the launch traced here: 1300 us
  waiting for transfers between devices  964 us (74%)
  matrix products  107 us (8%)
  blocking collectives  98.6 us (8%)
  other arithmetic  56.5 us (4%)
  local copies, waits for them, and re-layouts  49.1 us (4%)
  between operations  21 us (2%)
    unnamed x19, waiting for transfers between devices  184 us
    reduce_scatter x1, waiting for transfers between devices, on_device(): lax.psum_scatter(grad_ada, 'dp', scatter_dimension=1, tiled=True)  178 us
    reduce_scatter x1, waiting for transfers between devices, on_device(): lax.psum_scatter(grad_up[None], 'dp', scatter_dimension=1, tiled=True)  106 us
    all_gather x1, waiting for transfers between devices, on_device(): lax.all_gather(low_ada, 'dp', axis=1, tiled=True)  89.6 us
    reduce_scatter x1, waiting for transfers between devices, on_device(): lax.psum_scatter(grad_down[None], 'dp', scatter_dimension=1, tiled=True)  75.3 us
    all_gather x1, waiting for transfers between devices, on_device(): lax.all_gather(low_up, 'dp', axis=1, tiled=True)  51.5 us
    all_gather x1, waiting for transfers between devices, on_device(): lax.all_gather(low_down, 'dp', axis=1, tiled=True)  49.9 us
    reduce_scatter x1, waiting for transfers between devices, on_device(): lax.psum_scatter(attn_terms, 'tensor', scatter_dimension=1, tiled=True)  46.1 us
  transfers between devices with their start and end apart: 17, of which 16 were waited for; matrix products, arithmetic and copies ran while one was open for 8% of the time, Pallas kernels for 0%

commit v1 on v0

v1 whole, which is shorter than its diff:
```python
import jax
import jax.numpy as jnp
import numpy as np
from jax import lax
from jax.sharding import PartitionSpec as P

HEAD_DIM = 72
STEP = 10

EPS_NORM = 1e-06
CLIP_NORM = 1.0
LEARN_RATE = 0.05
WEIGHT_DECAY = 0.1
BETA_ONE = 0.9
BETA_TWO = 0.999
EPS_ADAM = 1e-08

LOW = jnp.bfloat16
WIDE = jnp.float32


def bit_count(size):
    return size.bit_length() - 1


def flip(value, axis, size, bit):
    return lax.ppermute(value, axis, [(i, i ^ (1 << bit)) for i in range(size)])


def gather_rel(value, axis, size):
    for bit in reversed(range(bit_count(size))):
        value = jnp.concatenate([value, flip(value, axis, size, bit)], axis=0)
    return value


def scatter_rel(value, axis, size):
    for bit in range(bit_count(size)):
        half = value.shape[0] // 2
        moved = flip(value[half:].astype(LOW), axis, size, bit)
        value = value[:half] + moved.astype(WIDE)
    return value


def exchange_rel(value, axis, size):
    lead = 1
    value = value[None]
    for bit in range(bit_count(size)):
        half = value.shape[1] // 2
        moved = flip(value[:, half:], axis, size, bit)
        value = jnp.stack([value[:, :half], moved], axis=1)
        lead *= 2
        value = value.reshape((lead, half) + value.shape[3:])
    return value[:, 0]


def sum_all(value, axis, size):
    for bit in range(bit_count(size)):
        value = value + flip(value, axis, size, bit)
    return value


def reversed_bits(size):
    bits = bit_count(size)
    return np.array([int(format(i, f"0{bits}b")[::-1], 2) if bits else 0 for i in range(size)])


def selection(index, size, width):
    block = width // size
    place = np.arange(width)
    source = (index ^ jnp.asarray(reversed_bits(size)[place // block], jnp.int32)) * block
    source = source + jnp.asarray(place % block, jnp.int32)
    return (lax.broadcasted_iota(jnp.int32, (width, width), 0) == source[None, :]).astype(LOW)


def matmul(left, right, dims):
    return lax.dot_general(left, right, (dims, ((), ())), preferred_element_type=WIDE)


def normalize(values):
    centre = values - jnp.mean(values, axis=-1, keepdims=True)
    spread = jnp.mean(centre * centre, axis=-1, keepdims=True)
    inverse = lax.rsqrt(spread + EPS_NORM)
    return centre * inverse, inverse


def normalize_back(normed, inverse, grad):
    mean_grad = jnp.mean(grad, axis=-1, keepdims=True)
    mean_both = jnp.mean(grad * normed, axis=-1, keepdims=True)
    return inverse * (grad - mean_grad - normed * mean_both)


def gelu_tanh(values):
    return jax.nn.gelu(values, approximate=True)


def to_blocks(stacked, block_rows):
    return stacked.reshape((-1, block_rows) + stacked.shape[1:])


def attend(queries, key_rows, values, block_rows):
    score_scale = HEAD_DIM ** (-0.5)

    def forward_block(query_part):
        scores = (
            jnp.einsum("qhe,khe->hqk", query_part, key_rows, preferred_element_type=WIDE)
            * score_scale
        )
        row_peak = jnp.max(scores, axis=-1, keepdims=True)
        exponent = jnp.exp(scores - row_peak)
        row_total = jnp.sum(exponent, axis=-1, keepdims=True)
        probability = (exponent / row_total).astype(LOW)
        mixture = jnp.einsum("hqk,khe->qhe", probability, values, preferred_element_type=WIDE)
        return (mixture.astype(LOW), (row_peak + jnp.log(row_total))[..., 0])

    mixed, log_totals = lax.map(forward_block, to_blocks(queries, block_rows))
    return mixed.reshape(queries.shape), log_totals


def attend_back(queries, key_rows, values, log_totals, grad_attended, block_rows):
    score_scale = HEAD_DIM ** (-0.5)

    def backward_block(carried, sample):
        grad_keys, grad_values = carried
        query_part, grad_part, log_part = sample
        scores = (
            jnp.einsum("qhe,khe->hqk", query_part, key_rows, preferred_element_type=WIDE)
            * score_scale
        )
        probability = jnp.exp(scores - log_part[..., None])
        grad_probability = jnp.einsum(
            "qhe,khe->hqk", grad_part, values, preferred_element_type=WIDE
        )
        row_inner = jnp.sum(probability * grad_probability, axis=-1, keepdims=True)
        grad_scores = (probability * (grad_probability - row_inner)).astype(LOW)
        grad_query = (
            jnp.einsum("hqk,khe->qhe", grad_scores, key_rows, preferred_element_type=WIDE)
            * score_scale
        )
        grad_keys = (
            grad_keys
            + jnp.einsum("hqk,qhe->khe", grad_scores, query_part, preferred_element_type=WIDE)
            * score_scale
        )
        grad_values = grad_values + jnp.einsum(
            "hqk,qhe->khe", probability.astype(LOW), grad_part, preferred_element_type=WIDE
        )
        return ((grad_keys, grad_values), grad_query.astype(LOW))

    zero_grad = jnp.zeros(key_rows.shape, WIDE)
    (grad_keys, grad_values), grad_queries = lax.scan(
        backward_block,
        (zero_grad, zero_grad),
        (to_blocks(queries, block_rows), to_blocks(grad_attended, block_rows), log_totals),
    )
    return (
        grad_queries.reshape(queries.shape),
        grad_keys.astype(LOW),
        grad_values.astype(LOW),
    )


def adam_update(weight, gradient, moment, square, clip_factor):
    clipped = gradient * clip_factor
    moment_new = BETA_ONE * moment + (1.0 - BETA_ONE) * clipped
    square_new = BETA_TWO * square + (1.0 - BETA_TWO) * clipped * clipped
    mean_hat = moment_new / (1.0 - BETA_ONE**STEP)
    square_hat = square_new / (1.0 - BETA_TWO**STEP)
    weight_new = weight - LEARN_RATE * (
        mean_hat / (jnp.sqrt(square_hat) + EPS_ADAM) + WEIGHT_DECAY * weight
    )
    return (weight_new, moment_new, square_new)


def on_device(
    dp,
    tp,
    tokens,
    conditioning,
    out_grad,
    qkv_weight,
    out_weight,
    up_weight,
    down_weight,
    ada_weight,
    qkv_moment,
    out_moment,
    up_moment,
    down_moment,
    ada_moment,
    qkv_square,
    out_square,
    up_square,
    down_square,
    ada_square,
):
    width = tokens.shape[-1]
    own_rows = tokens.shape[1]
    heads_width = out_weight.shape[-1]
    here = lax.axis_index("dp")
    select = selection(here, dp, width)

    both = jnp.concatenate(
        [
            matmul(tokens[0], select, ((1,), (0,))).astype(LOW),
            matmul(out_grad[0], select, ((1,), (0,))).astype(LOW),
        ],
        axis=1,
    )
    both = gather_rel(both, "tensor", tp)
    tokens_all = both[:, :width].astype(WIDE)
    grad_all = both[:, width:].astype(WIDE)

    low_qkv = jnp.moveaxis(qkv_weight.astype(LOW), 0, 1).reshape(qkv_weight.shape[1], -1)
    full_qkv = gather_rel(low_qkv, "dp", dp)
    full_out = gather_rel(out_weight.astype(LOW), "dp", dp)
    full_up = gather_rel(up_weight.astype(LOW), "dp", dp)
    full_down = gather_rel(down_weight.astype(LOW), "dp", dp)
    low_ada = ada_weight.astype(LOW)

    signal, silu_back = jax.vjp(jax.nn.silu, conditioning)
    signal_all = gather_rel(signal.astype(LOW), "dp", dp)
    mod_terms = jnp.einsum("pi,kni->pkn", signal_all, low_ada, preferred_element_type=WIDE)
    mod_terms = sum_all(mod_terms, "tensor", tp)
    modulation = exchange_rel(mod_terms, "dp", dp)
    modulation = jnp.moveaxis(modulation, 0, 1).reshape(6, 1, width)
    shift_one, scale_one, gate_one, shift_two, scale_two, gate_two = modulation

    norm_one, inverse_one = normalize(tokens_all)
    normed_one = (norm_one * (1.0 + scale_one) + shift_one).astype(LOW)
    projected = matmul(normed_one, full_qkv, ((1,), (0,))).astype(LOW)
    length = projected.shape[0]
    block_rows = min(512, length)
    heads_split = projected.reshape(length, 3, heads_width // HEAD_DIM, HEAD_DIM)
    queries, key_rows, values = heads_split[:, 0], heads_split[:, 1], heads_split[:, 2]
    mixed, log_totals = attend(queries, key_rows, values, block_rows)
    attended = mixed.reshape(length, heads_width)
    attn_terms = matmul(attended, full_out, ((1,), (1,)))

    def sum_half(terms):
        half = terms.shape[0] // 2
        total = terms[:half] + flip(terms[half:].astype(LOW), "tensor", tp, 0).astype(WIDE)
        for bit in range(1, bit_count(tp)):
            sent = total.astype(LOW)
            moved = flip(sent, "tensor", tp, bit)
            blocks = moved.reshape((-1, 2, own_rows << (bit_count(tp) - 1 - bit), width))
            moved = blocks[:, ::-1].reshape(moved.shape)
            total = sent.astype(WIDE) + moved.astype(WIDE)
        return total

    half = length // 2
    attn_rows = sum_half(attn_terms)
    middle = tokens_all[:half] + gate_one * attn_rows
    norm_two, inverse_two = normalize(middle)
    normed_two = (norm_two * (1.0 + scale_two) + shift_two).astype(LOW)
    seq_two = jnp.concatenate([normed_two, flip(normed_two, "tensor", tp, 0)], axis=0)

    pre_act = matmul(seq_two, full_up, ((1,), (0,)))
    activated, gelu_back = jax.vjp(gelu_tanh, pre_act)
    hidden = activated.astype(LOW)
    mlp_terms = matmul(hidden, full_down, ((1,), (1,)))
    mlp_rows = scatter_rel(mlp_terms, "tensor", tp)
    block_out = (middle[:own_rows] + gate_two * mlp_rows).astype(LOW)
    block_out = matmul(block_out, select, ((1,), (1,))).astype(LOW)
    grad_gate_two = jnp.sum(grad_all[:own_rows] * mlp_rows, axis=0)

    grad_mlp = (grad_all * gate_two).astype(LOW)
    grad_down = matmul(grad_mlp, hidden, ((0,), (0,)))
    grad_hidden = matmul(grad_mlp, full_down, ((1,), (0,)))
    grad_pre = gelu_back(grad_hidden)[0].astype(LOW)
    grad_up = matmul(seq_two, grad_pre, ((0,), (0,)))
    grad_two_terms = matmul(grad_pre, full_up, ((1,), (1,)))
    summed_down = scatter_rel(grad_down, "dp", dp)
    summed_up = scatter_rel(grad_up, "dp", dp)
    grad_normed_two = sum_half(grad_two_terms)
    grad_shift_two = jnp.sum(grad_normed_two[:own_rows], axis=0)
    grad_scale_two = jnp.sum((grad_normed_two * norm_two)[:own_rows], axis=0)
    grad_middle = grad_all[:half] + normalize_back(
        norm_two, inverse_two, grad_normed_two * (1.0 + scale_two)
    )
    grad_gate_one = jnp.sum((grad_middle * attn_rows)[:own_rows], axis=0)

    grad_attn = (grad_middle * gate_one).astype(LOW)
    grad_attn = jnp.concatenate([grad_attn, flip(grad_attn, "tensor", tp, 0)], axis=0)
    grad_out = matmul(grad_attn, attended, ((0,), (0,)))
    summed_out = scatter_rel(grad_out, "dp", dp)
    grad_attended = matmul(grad_attn, full_out, ((1,), (0,))).astype(LOW)
    grad_parts = attend_back(
        queries, key_rows, values, log_totals, grad_attended.reshape(queries.shape), block_rows
    )
    grad_projected = jnp.stack(grad_parts, axis=1).reshape(length, 3 * heads_width)
    grad_qkv = matmul(normed_one, grad_projected, ((0,), (0,)))
    summed_qkv = scatter_rel(grad_qkv, "dp", dp)
    grad_one_terms = matmul(grad_projected, full_qkv, ((1,), (1,)))
    grad_normed_one = scatter_rel(grad_one_terms, "tensor", tp)
    input_grad = grad_middle[:own_rows] + normalize_back(
        norm_one[:own_rows], inverse_one[:own_rows], grad_normed_one * (1.0 + scale_one)
    )
    coarse = input_grad.astype(LOW)
    fine = (input_grad - coarse.astype(WIDE)).astype(LOW)
    input_grad = matmul(coarse, select, ((1,), (1,))) + matmul(fine, select, ((1,), (1,)))

    grad_shift_one = jnp.sum(grad_one_terms, axis=0)
    grad_scale_one = jnp.sum(grad_one_terms * norm_one, axis=0)
    grad_mod = jnp.stack(
        [
            grad_shift_one,
            grad_scale_one,
            grad_gate_one,
            grad_shift_two,
            grad_scale_two,
            grad_gate_two,
        ]
    )
    grad_mod = sum_all(grad_mod, "tensor", tp).astype(LOW)
    grad_mod = jnp.moveaxis(grad_mod.reshape(6, dp, width // dp), 1, 0)
    grad_mod = exchange_rel(grad_mod, "dp", dp)
    summed_ada = jnp.einsum("pkn,pi->kni", grad_mod, signal_all, preferred_element_type=WIDE)
    grad_signal = jnp.einsum("pkn,kni->pi", grad_mod, low_ada, preferred_element_type=WIDE)
    for bit in range(bit_count(dp)):
        part = grad_signal.shape[0] // 2
        grad_signal = grad_signal[:part] + flip(grad_signal[part:], "dp", dp, bit)
    cond_grad = silu_back(grad_signal)[0]

    summed_qkv = jnp.moveaxis(summed_qkv.reshape(-1, 3, heads_width), 1, 0)
    total = jnp.sum(summed_qkv * summed_qkv) + jnp.sum(summed_out * summed_out)
    total = total + jnp.sum(summed_up * summed_up) + jnp.sum(summed_down * summed_down)
    total = total + jnp.sum(summed_ada * summed_ada)
    total = sum_all(sum_all(total, "tensor", tp), "dp", dp)
    grad_norm = jnp.sqrt(total)
    clip_factor = CLIP_NORM / jnp.maximum(grad_norm, CLIP_NORM)
    qkv = adam_update(qkv_weight, summed_qkv, qkv_moment, qkv_square, clip_factor)
    out = adam_update(out_weight, summed_out, out_moment, out_square, clip_factor)
    up = adam_update(up_weight, summed_up, up_moment, up_square, clip_factor)
    down = adam_update(down_weight, summed_down, down_moment, down_square, clip_factor)
    ada = adam_update(ada_weight, summed_ada, ada_moment, ada_square, clip_factor)
    return (
        block_out[None],
        input_grad[None],
        cond_grad,
        grad_norm,
        *(new for group in zip(qkv, out, up, down, ada) for new in group),
    )


def solution(mesh):
    dp, tp = mesh.shape["dp"], mesh.shape["tensor"]
    rows = P("dp", "tensor", None)
    plain = P("dp", "tensor")
    stacked = P(None, "dp", "tensor")
    weights = (stacked, plain, plain, plain, stacked)

    def step(*arrays):
        return on_device(dp, tp, *arrays)

    return jax.shard_map(
        step,
        mesh=mesh,
        in_specs=(rows, plain, rows) + weights * 3,
        out_specs=(rows, rows, plain, P()) + weights * 3,
        check_vma=False,
    )
```

time: 1310 us -> 564 us (0.43)
  waiting for transfers between devices: 964 us -> 194 us
  blocking collectives: 98.6 us -> 0 us
  starting transfers between devices: 1.81 us -> 63.7 us
  local copies, waits for them, and re-layouts: 49.1 us -> 97.9 us
  other arithmetic: 56.5 us -> 99.5 us
  matrix products: 107 us -> 91 us
    reduce_scatter x7 -> x0, waiting for transfers between devices: 477 us -> none  [the longest x1 178 us: on_device(): lax.psum_scatter(grad_ada, 'dp', scatter_dimension=1, tiled=True)]
    all_gather x8 -> x0, waiting for transfers between devices: 303 us -> none  [the longest x1 89.6 us: on_device(): lax.all_gather(low_ada, 'dp', axis=1, tiled=True)]
    ppermute x0 -> x57, waiting for transfers between devices: none -> 194 us  [flip(): return lax.ppermute(value, axis, [(i, i ^ 1 << bit) for i in range(size)])]
    unnamed x19 -> x0, waiting for transfers between devices: 184 us -> none
    ppermute x0 -> x57, starting transfers between devices: none -> 63.7 us  [flip(): return lax.ppermute(value, axis, [(i, i ^ 1 << bit) for i in range(size)])]
    psum x3 -> x0, blocking collectives: 61.9 us -> none  [the longest x1 39.3 us: on_device(): total_squares = lax.psum(local_squares, ('dp', 'tensor'))]
    all_gather x1 -> x0, blocking collectives: 36.7 us -> none  [on_device(): lax.all_gather(low_out, 'dp', axis=1, tiled=True)]
    rev x0 -> x2, local copies, waits for them, and re-layouts: none -> 21.8 us  [sum_half(): moved = blocks[:, ::-1].reshape(moved.shape)]
  transfers between devices with their start and end apart: 17 -> 57, of which waited for: 16 -> 26; matrix products, arithmetic and copies ran while one was open for 8% -> 40% of each run, Pallas kernels for 0% -> 0%
where the time goes in v1:
time: 564 us; the launch traced here: 557 us
  waiting for transfers between devices  194 us (34%)
  other arithmetic  99.5 us (18%)
  local copies, waits for them, and re-layouts  97.9 us (17%)
  matrix products  91 us (16%)
  starting transfers between devices  63.7 us (11%)
  between operations  10.1 us (2%)
    ppermute x57, waiting for transfers between devices, flip(): return lax.ppermute(value, axis, [(i, i ^ 1 << bit) for i in range(size)])  194 us
    ppermute x57, starting transfers between devices, flip(): return lax.ppermute(value, axis, [(i, i ^ 1 << bit) for i in range(size)])  63.7 us
    dot_general x17, matrix products, matmul(): lax.dot_general(left, right, (dims, ((), ())), preferred_element_type=WIDE)  63.3 us
    unnamed x219, local copies, waits for them, and re-layouts  24.7 us
    rev x2, local copies, waits for them, and re-layouts, sum_half(): moved = blocks[:, ::-1].reshape(moved.shape)  21.8 us
    concatenate x12, other arithmetic, gather_rel(): value = jnp.concatenate([value, flip(value, axis, size, bit)], axis=0)  20 us
    slice x18, local copies, waits for them, and re-layouts, scatter_rel(): moved = flip(value[half:].astype(LOW), axis, size, bit)  13.8 us
    sub x5, other arithmetic, adam_update(): weight - LEARN_RATE * (mean_hat / (jnp.sqrt(square_hat) + EPS_ADAM) + WEI...  13.6 us
  transfers between devices with their start and end apart: 57, of which 26 were waited for; matrix products, arithmetic and copies ran while one was open for 40% of the time, Pallas kernels for 0%

profile of v1, /device:TPU:0, one launch (start us, length us, event | category | flops | bytes accessed | tf_op | source)
XLA Modules:
  0.0 556.6 jit_solution(371072113372719435)
XLA Ops:
  25.3 9.3 %collective-permute-done = bf16[256,2304]{0,1:T(8,128)(2,1)S(1)} collective-permute-done((bf16[256,2304]{0,1:T(8,128)(2,1)}, bf16[256,2304]{0,1:T(8,128)(2,1)S(1)}, u32[]{:S(2)}, u32[]{:S(2)}) %collective-permute-start) | collective-permute-done | bytes 1179680 | tf_op jit(solution)/shard_map/ppermute | solution.py:27
  42.8 10.8 %collective-permute-done.8 = f32[2,2,6,144]{3,1,2,0:T(2,128)} collective-permute-done((f32[2,2,6,144]{3,1,2,0:T(2,128)S(1)}, f32[2,2,6,144]{3,1,2,0:T(2,128)}, u32[]{:S(2)}, u32[]{:S(2)}) %collective-permute-start.8) | collective-permute-done | bytes 13856 | tf_op jit(solution)/shard_map/ppermute | solution.py:27
  71.4 10.1 %collective-permute-done.12 = bf16[576,864]{1,0:T(8,128)(2,1)} collective-permute-done((bf16[576,864]{1,0:T(8,128)(2,1)}, bf16[576,864]{1,0:T(8,128)(2,1)}, u32[]{:S(2)}, u32[]{:S(2)}) %collective-permute-start.12) | collective-permute-done | bytes 995360 | tf_op jit(solution)/shard_map/ppermute | solution.py:27
  83.8 6.5 %pad_maximum_fusion = bf16[1024,2304]{0,1:T(8,128)(2,1)S(1)} fusion(bf16[512,2304]{0,1:T(8,128)(2,1)} %collective-permute-done.1, bf16[256,2304]{0,1:T(8,128)(2,1)S(1)} %collective-permute-done, bf16[256,1152]{0,1:T(8,128)(2,1)S(1)} %fusion.71, bf16[256,1152]{0,1:T(8,128)(2,1)S(1)} %fusion.74), kind=kLoop, calls=%fused_computation.60 | loop fusion | flops 18874368 | bytes 9437184 | tf_op jit(solution)/shard_map/concatenate | solution.py:32
  97.0 12.4 %while.27 = (s32[]{:T(128)}, bf16[2,512,4,72]{1,3,2,0:T(8,128)(2,1)S(1)}, f32[2,4,512]{2,1,0:T(4,128)}, bf16[2,512,4,72]{1,3,2,0:T(8,128)(2,1)S(1)}, bf16[1024,4...) while((s32[]{:T(128)}, bf16[2,512,4,72]{1,3,2,0:T(8,128)(2,1)S(1)}, ...), condition=%wide.region_5.6_spmd, body=%wide.region_2.5_spmd.sunk | while | flops 622999552 | bytes 27000928 | solution.py:115
  117.7 15.3 %collective-permute-done.19 = bf16[144,1152]{1,0:T(8,128)(2,1)S(1)} collective-permute-done((bf16[144,1152]{1,0:T(8,128)(2,1)S(1)}, bf16[144,1152]{1,0:T(8,128)(2,1)S(1)}, u32[]{:S(2)}, u32[]{:S(2)}) %collective-permute-start.19) | collective-permute-done | bytes 331808 | tf_op jit(solution)/shard_map/ppermute | solution.py:27
  143.6 13.9 %collective-permute-done.20 = bf16[288,1152]{1,0:T(8,128)(2,1)} collective-permute-done((bf16[288,1152]{1,0:T(8,128)(2,1)}, bf16[288,1152]{1,0:T(8,128)(2,1)}, u32[]{:S(2)}, u32[]{:S(2)}) %collective-permute-start.20) | collective-permute-done | bytes 663584 | tf_op jit(solution)/shard_map/ppermute | solution.py:27
  160.5 7.1 %slice_convert_fusion.4 = (f32[1024,1152]{0,1:T(8,128)}, f32[1024,1152]{0,1:T(8,128)}) fusion(bf16[1024,2304]{0,1:T(8,128)(2,1)} %copy-done.2), kind=kLoop, calls=%fused_computation.95 | loop fusion | flops 2359296 | bytes 14155776 | tf_op jit(solution)/shard_map/convert_element_type | solution.py:211
  173.3 10.5 %rev.6 = bf16[1,2,256,1152]{2,1,3,0:T(2,128)(2,1)S(1)} reverse(bf16[1,2,256,1152]{2,1,3,0:T(2,128)(2,1)} %reshape.199), dimensions={1} | reverse | bytes 2359296 | tf_op jit(solution)/shard_map/rev | solution.py:246
  199.5 11.5 %collective-permute-done.23 = bf16[288,1152]{1,0:T(8,128)(2,1)} collective-permute-done((bf16[288,1152]{1,0:T(8,128)(2,1)}, bf16[288,1152]{1,0:T(8,128)(2,1)}, u32[]{:S(2)}, u32[]{:S(2)}) %collective-permute-start.23) | collective-permute-done | bytes 663584 | tf_op jit(solution)/shard_map/ppermute | solution.py:27
  213.0 6.0 %fusion.82 = f32[1024,1152]{1,0:T(8,128)S(1)} fusion(bf16[512,1152]{0,1:T(8,128)(2,1)} %collective-permute-done.18, bf16[512,1152]{0,1:T(8,128)(2,1)} %get-tuple-element.354, bf16[576,1152]{1,0:T(8,128)(2,1)} %collective-permute-done.21, bf16[288,1152]{1,0:T(8,128)(2,1)} %collective-permute-done.20, bf16[144,1152]{1,0:T(8,128)(2,1)S(1)} %copy-done.44, ...), kind=kOutput, calls=%fused_computation.121 | convolution fusion | flops 2733244416 | bytes 9732096 | tf_op jit(solution)/shard_map/dot_general | solution.py:76
  222.6 20.6 %collective-permute-done.24 = bf16[576,1152]{1,0:T(8,128)(2,1)S(1)} collective-permute-done((bf16[576,1152]{1,0:T(8,128)(2,1)S(1)}, bf16[576,1152]{1,0:T(8,128)(2,1)S(1)}, u32[]{:S(2)}, u32[]{:S(2)}) %collective-permute-start.24) | collective-permute-done | bytes 1327136 | tf_op jit(solution)/shard_map/ppermute | solution.py:27
  249.0 9.2 %fusion.51 = bf16[1024,1152]{1,0:T(8,128)(2,1)} fusion(f32[1024,1152]{1,0:T(8,128)S(1)} %fusion.82, f32[1152]{0:T(1024)S(1)} %copy-done.93, bf16[1024,2304]{0,1:T(8,128)(2,1)S(1)} %bitcast.201, bf16[576,1152]{1,0:T(8,128)(2,1)S(1)} %collective-permute-done.24, bf16[288,1152]{1,0:T(8,128)(2,1)} %collective-permute-done.23, ...), kind=kOutput, calls=%fused_computation.59 | convolution fusion | flops 2755657728 | bytes 12099584 | tf_op jit(solution)/shard_map/dot_general | solution.py:76
  258.2 5.6 %fusion.102 = f32[1024,1152]{0,1:T(8,128)S(1)} fusion(bf16[1024,1152]{1,0:T(8,128)(2,1)} %fusion.51, bf16[576,1152]{1,0:T(8,128)(2,1)} %collective-permute-done.21, bf16[288,1152]{1,0:T(8,128)(2,1)} %collective-permute-done.20, bf16[144,1152]{1,0:T(8,128)(2,1)S(1)} %copy-done.44, bf16[144,1152]{1,0:T(8,128)(2,1)S(1)} %copy-done.28), kind=kOutput, calls=%fused_computation.195 | convolution fusion | flops 2728525824 | bytes 9732096 | tf_op jit(solution)/shard_map/dot_general | solution.py:76
  274.5 5.9 %collective-permute-done.49 = bf16[576,1152]{1,0:T(8,128)(2,1)S(1)} collective-permute-done((bf16[576,1152]{1,0:T(8,128)(2,1)S(1)}, bf16[576,1152]{1,0:T(8,128)(2,1)S(1)}, u32[]{:S(2)}, u32[]{:S(2)}) %collective-permute-start.49) | collective-permute-done | bytes 1327136 | tf_op jit(solution)/shard_map/ppermute | solution.py:27
  281.1 27.3 %collective-permute-done.46 = bf16[576,1152]{1,0:T(8,128)(2,1)S(1)} collective-permute-done((bf16[576,1152]{1,0:T(8,128)(2,1)S(1)}, bf16[576,1152]{1,0:T(8,128)(2,1)S(1)}, u32[]{:S(2)}, u32[]{:S(2)}) %collective-permute-start.46) | collective-permute-done | bytes 1327136 | tf_op jit(solution)/shard_map/ppermute | solution.py:27
  319.8 11.3 %rev.7 = bf16[1,2,256,1152]{2,1,3,0:T(2,128)(2,1)} reverse(bf16[1,2,256,1152]{2,1,3,0:T(2,128)(2,1)} %reshape.200), dimensions={1} | reverse | bytes 2359296 | tf_op jit(solution)/shard_map/rev | solution.py:246
  345.3 12.9 %collective-permute-done.48 = bf16[144,1152]{1,0:T(8,128)(2,1)S(1)} collective-permute-done((bf16[144,1152]{1,0:T(8,128)(2,1)S(1)}, bf16[144,1152]{1,0:T(8,128)(2,1)S(1)}, u32[]{:S(2)}, u32[]{:S(2)}) %collective-permute-start.48) | collective-permute-done | bytes 331808 | tf_op jit(solution)/shard_map/ppermute | solution.py:27
  370.1 22.4 %while.28 = (s32[]{:T(128)}, f32[1024,4,72]{0,2,1:T(8,128)S(1)}, f32[1024,4,72]{0,2,1:T(8,128)S(1)}, bf16[2,512,4,72]{1,3,2,0:T(8,128)(2,1)}, bf16[2,512,4,72]{1...) while((s32[]{:T(128)}, f32[1024,4,72]{0,2,1:T(8,128)S(1)}, ...), condition=%wide.region_12.13_spmd.clone, body=%wide.region_10.12_spmd.clone.sunk | while | flops 1536882688 | bytes 80371976 | solution.py:150
  408.8 6.1 %copy.159 = f32[1024,1152]{0,1:T(8,128)} copy(f32[1024,1152]{1,0:T(8,128)} %get-tuple-element.393) | data formatting | bytes 9437184 | tf_op jit(solution)/shard_map/dot_general | solution.py:76
  426.7 6.2 %multiply_reduce_fusion.2 = (f32[1152]{0:T(1024)S(1)}, f32[1024,1152]{0,1:T(8,128)}) fusion(f32[1024,1152]{0,1:T(8,128)} %copy.159, f32[1024]{0:T(1024)S(1)} %copy-done.78, f32[1024]{0:T(1024)S(1)} %copy-done.68, bf16[1024,2304]{0,1:T(8,128)(2,1)} %copy-done.2), kind=kLoop, calls=%fused_computation.61 | loop fusion | flops 5897088 | bytes 11809280 | tf_op jit(solution)/shard_map/reduce_sum | solution.py:303
  443.1 8.5 %collective-permute-done.40 = bf16[576,864]{1,0:T(8,128)(2,1)} collective-permute-done((bf16[576,864]{1,0:T(8,128)(2,1)}, bf16[576,864]{1,0:T(8,128)(2,1)}, u32[]{:S(2)}, u32[]{:S(2)}) %collective-permute-start.40) | collective-permute-done | bytes 995360 | tf_op jit(solution)/shard_map/ppermute | solution.py:27
  467.9 6.7 %collective-permute-done.41 = bf16[288,864]{1,0:T(8,128)(2,1)} collective-permute-done((bf16[288,864]{1,0:T(8,128)(2,1)}, bf16[288,864]{1,0:T(8,128)(2,1)}, u32[]{:S(2)}, u32[]{:S(2)}) %collective-permute-start.41) | collective-permute-done | bytes 497696 | tf_op jit(solution)/shard_map/ppermute | solution.py:27
  480.7 19.5 %collective-permute-done.42 = bf16[144,864]{0,1:T(8,128)(2,1)S(1)} collective-permute-done((bf16[144,864]{0,1:T(8,128)(2,1)S(1)}, bf16[144,864]{0,1:T(8,128)(2,1)S(1)}, u32[]{:S(2)}, u32[]{:S(2)}) %collective-permute-start.42) | collective-permute-done | bytes 248864 | tf_op jit(solution)/shard_map/ppermute | solution.py:27
  (528 shorter events, 304.8 us)
Async XLA Ops:
  5.0 29.7 %collective-permute-start = (bf16[256,2304]{0,1:T(8,128)(2,1)}, bf16[256,2304]{0,1:T(8,128)(2,1)S(1)}, u32[]{:S(2)}, u32[]{:S(2)}) collective-permute-start(bf16[256,2304]{0,1:T(8,128)(2,1)} %pad_maximum_fusion.15), channel_id=1, source_target_pairs={{0,2},{1,3},{2,0},{3,1},{4,6},{5,7},{6,4},{7,5},{8,10},{9,11},{10,... | collective-permute-start | bytes 3538952 | tf_op jit(solution)/shard_map/ppermute | solution.py:27
  18.3 40.4 %collective-permute-start.13 = (bf16[144,288]{1,0:T(8,128)(2,1)S(1)}, bf16[144,288]{1,0:T(8,128)(2,1)}, u32[]{:S(2)}, u32[]{:S(2)}) collective-permute-start(bf16[144,288]{1,0:T(8,128)(2,1)S(1)} %convert_element_type.212), channel_id=1, source_target_pairs={{0,16},{4,20},{8,24},{12,28},{16,0},{20,4},{24,8},{28,12},{1,17},{... | collective-permute-start | bytes 248840 | tf_op jit(solution)/shard_map/ppermute | solution.py:27
  36.3 47.5 %collective-permute-start.1 = (bf16[512,2304]{0,1:T(8,128)(2,1)}, bf16[512,2304]{0,1:T(8,128)(2,1)}, u32[]{:S(2)}, u32[]{:S(2)}) collective-permute-start(bf16[512,2304]{0,1:T(8,128)(2,1)} %pad_maximum_fusion.3), channel_id=1, source_target_pairs={{0,1},{1,0},{2,3},{3,2},{4,5},{5,4},{6,7},{7,6},{8,9},{9,8},{10,11... | collective-permute-start | bytes 7077896 | tf_op jit(solution)/shard_map/ppermute | solution.py:27
  55.5 26.1 %collective-permute-start.12 = (bf16[576,864]{1,0:T(8,128)(2,1)}, bf16[576,864]{1,0:T(8,128)(2,1)}, u32[]{:S(2)}, u32[]{:S(2)}) collective-permute-start(bf16[576,864]{1,0:T(8,128)(2,1)} %pad_maximum_fusion.16), channel_id=1, source_target_pairs={{0,4},{4,0},{8,12},{12,8},{16,20},{20,16},{24,28},{28,24},{1,5},{5... | collective-permute-start | bytes 2985992 | tf_op jit(solution)/shard_map/ppermute | solution.py:27
  68.4 41.8 %collective-permute-start.15 = (bf16[576,288]{1,0:T(8,128)(2,1)}, bf16[576,288]{1,0:T(8,128)(2,1)}, u32[]{:S(2)}, u32[]{:S(2)}) collective-permute-start(bf16[576,288]{1,0:T(8,128)(2,1)} %pad_maximum_fusion.25), channel_id=1, source_target_pairs={{0,4},{4,0},{8,12},{12,8},{16,20},{20,16},{24,28},{28,24},{1,5},{5... | collective-permute-start | bytes 995336 | tf_op jit(solution)/shard_map/ppermute | solution.py:27
  114.7 25.0 %collective-permute-start.16 = (bf16[512,1152]{0,1:T(8,128)(2,1)}, bf16[512,1152]{0,1:T(8,128)(2,1)}, u32[]{:S(2)}, u32[]{:S(2)}) collective-permute-start(bf16[512,1152]{0,1:T(8,128)(2,1)} %slice.501), channel_id=1, source_target_pairs={{0,1},{1,0},{2,3},{3,2},{4,5},{5,4},{6,7},{7,6},{8,9},{9,8},{10,11... | collective-permute-start | bytes 3538952 | tf_op jit(solution)/shard_map/ppermute | solution.py:27
  134.0 23.6 %collective-permute-start.20 = (bf16[288,1152]{1,0:T(8,128)(2,1)}, bf16[288,1152]{1,0:T(8,128)(2,1)}, u32[]{:S(2)}, u32[]{:S(2)}) collective-permute-start(bf16[288,1152]{1,0:T(8,128)(2,1)} %pad_maximum_fusion.18), channel_id=1, source_target_pairs={{0,8},{4,12},{8,0},{12,4},{16,24},{20,28},{24,16},{28,20},{1,9},{5... | collective-permute-start | bytes 1990664 | tf_op jit(solution)/shard_map/ppermute | solution.py:27
  135.4 56.0 %collective-permute-start.22 = (bf16[144,1152]{1,0:T(8,128)(2,1)}, bf16[144,1152]{1,0:T(8,128)(2,1)}, u32[]{:S(2)}, u32[]{:S(2)}) collective-permute-start(bf16[144,1152]{1,0:T(8,128)(2,1)} %convert_element_type.221), channel_id=1, source_target_pairs={{0,16},{4,20},{8,24},{12,28},{16,0},{20,4},{24,8},{28,12},{1,17},{... | collective-permute-start | bytes 995336 | tf_op jit(solution)/shard_map/ppermute | solution.py:27
  142.0 27.5 %collective-permute-start.17 = (bf16[512,1152]{0,1:T(8,128)(2,1)S(1)}, bf16[512,1152]{0,1:T(8,128)(2,1)}, u32[]{:S(2)}, u32[]{:S(2)}) collective-permute-start(bf16[512,1152]{0,1:T(8,128)(2,1)S(1)} %fusion.78), channel_id=1, source_target_pairs={{0,2},{1,3},{2,0},{3,1},{4,6},{5,7},{6,4},{7,5},{8,10},{9,11},{10,... | collective-permute-start | bytes 3538952 | tf_op jit(solution)/shard_map/ppermute | solution.py:27
  159.8 53.1 %collective-permute-start.21 = (bf16[576,1152]{1,0:T(8,128)(2,1)}, bf16[576,1152]{1,0:T(8,128)(2,1)}, u32[]{:S(2)}, u32[]{:S(2)}) collective-permute-start(bf16[576,1152]{1,0:T(8,128)(2,1)} %pad_maximum_fusion.11), channel_id=1, source_target_pairs={{0,4},{4,0},{8,12},{12,8},{16,20},{20,16},{24,28},{28,24},{1,5},{5... | collective-permute-start | bytes 3981320 | tf_op jit(solution)/shard_map/ppermute | solution.py:27
  212.4 30.8 %collective-permute-start.24 = (bf16[576,1152]{1,0:T(8,128)(2,1)S(1)}, bf16[576,1152]{1,0:T(8,128)(2,1)S(1)}, u32[]{:S(2)}, u32[]{:S(2)}) collective-permute-start(bf16[576,1152]{1,0:T(8,128)(2,1)S(1)} %pad_maximum_fusion.12), channel_id=1, source_target_pairs={{0,4},{4,0},{8,12},{12,8},{16,20},{20,16},{24,28},{28,24},{1,5},{5... | collective-permute-start | bytes 3981320 | tf_op jit(solution)/shard_map/ppermute | solution.py:27
  248.4 32.0 %collective-permute-start.49 = (bf16[576,1152]{1,0:T(8,128)(2,1)S(1)}, bf16[576,1152]{1,0:T(8,128)(2,1)S(1)}, u32[]{:S(2)}, u32[]{:S(2)}) collective-permute-start(bf16[576,1152]{1,0:T(8,128)(2,1)S(1)} %slice.496), channel_id=1, source_target_pairs={{0,4},{4,0},{8,12},{12,8},{16,20},{20,16},{24,28},{28,24},{1,5},{5... | collective-permute-start | bytes 3981320 | tf_op jit(solution)/shard_map/ppermute | solution.py:27
  269.7 38.7 %collective-permute-start.46 = (bf16[576,1152]{1,0:T(8,128)(2,1)S(1)}, bf16[576,1152]{1,0:T(8,128)(2,1)S(1)}, u32[]{:S(2)}, u32[]{:S(2)}) collective-permute-start(bf16[576,1152]{1,0:T(8,128)(2,1)S(1)} %slice.497), channel_id=1, source_target_pairs={{0,4},{4,0},{8,12},{12,8},{16,20},{20,16},{24,28},{28,24},{1,5},{5... | collective-permute-start | bytes 3981320 | tf_op jit(solution)/shard_map/ppermute | solution.py:27
  271.8 38.2 %collective-permute-start.26 = (bf16[256,1152]{0,1:T(8,128)(2,1)S(1)}, bf16[256,1152]{0,1:T(8,128)(2,1)S(1)}, u32[]{:S(2)}, u32[]{:S(2)}) collective-permute-start(bf16[256,1152]{0,1:T(8,128)(2,1)S(1)} %slice.507), channel_id=1, source_target_pairs={{0,2},{1,3},{2,0},{3,1},{4,6},{5,7},{6,4},{7,5},{8,10},{9,11},{10,... | collective-permute-start | bytes 1769480 | tf_op jit(solution)/shard_map/ppermute | solution.py:27
  273.9 42.1 %collective-permute-start.28 = (bf16[512,1152]{0,1:T(8,128)(2,1)S(1)}, bf16[512,1152]{0,1:T(8,128)(2,1)}, u32[]{:S(2)}, u32[]{:S(2)}) collective-permute-start(bf16[512,1152]{0,1:T(8,128)(2,1)S(1)} %fusion.77), channel_id=1, source_target_pairs={{0,2},{1,3},{2,0},{3,1},{4,6},{5,7},{6,4},{7,5},{8,10},{9,11},{10,... | collective-permute-start | bytes 3538952 | tf_op jit(solution)/shard_map/ppermute | solution.py:27
  280.8 31.6 %collective-permute-start.50 = (bf16[288,1152]{1,0:T(8,128)(2,1)S(1)}, bf16[288,1152]{1,0:T(8,128)(2,1)S(1)}, u32[]{:S(2)}, u32[]{:S(2)}) collective-permute-start(bf16[288,1152]{1,0:T(8,128)(2,1)S(1)} %slice.503), channel_id=1, source_target_pairs={{0,8},{4,12},{8,0},{12,4},{16,24},{20,28},{24,16},{28,20},{1,9},{5... | collective-permute-start | bytes 1990664 | tf_op jit(solution)/shard_map/ppermute | solution.py:27
  309.8 28.8 %collective-permute-start.47 = (bf16[288,1152]{1,0:T(8,128)(2,1)}, bf16[288,1152]{1,0:T(8,128)(2,1)}, u32[]{:S(2)}, u32[]{:S(2)}) collective-permute-start(bf16[288,1152]{1,0:T(8,128)(2,1)} %slice.504), channel_id=1, source_target_pairs={{0,8},{4,12},{8,0},{12,4},{16,24},{20,28},{24,16},{28,20},{1,9},{5... | collective-permute-start | bytes 1990664 | tf_op jit(solution)/shard_map/ppermute | solution.py:27
  313.7 29.8 %collective-permute-start.51 = (bf16[144,1152]{1,0:T(8,128)(2,1)}, bf16[144,1152]{1,0:T(8,128)(2,1)}, u32[]{:S(2)}, u32[]{:S(2)}) collective-permute-start(bf16[144,1152]{1,0:T(8,128)(2,1)} %slice.510), channel_id=1, source_target_pairs={{0,16},{4,20},{8,24},{12,28},{16,0},{20,4},{24,8},{28,12},{1,17},{... | collective-permute-start | bytes 995336 | tf_op jit(solution)/shard_map/ppermute | solution.py:27
  401.0 31.9 %collective-permute-start.43 = (bf16[576,288]{0,1:T(8,128)(2,1)}, bf16[576,288]{0,1:T(8,128)(2,1)}, u32[]{:S(2)}, u32[]{:S(2)}) collective-permute-start(bf16[576,288]{0,1:T(8,128)(2,1)} %slice.509), channel_id=1, source_target_pairs={{0,4},{4,0},{8,12},{12,8},{16,20},{20,16},{24,28},{28,24},{1,5},{5... | collective-permute-start | bytes 995336 | tf_op jit(solution)/shard_map/ppermute | solution.py:27
  426.1 25.5 %collective-permute-start.40 = (bf16[576,864]{1,0:T(8,128)(2,1)}, bf16[576,864]{1,0:T(8,128)(2,1)}, u32[]{:S(2)}, u32[]{:S(2)}) collective-permute-start(bf16[576,864]{1,0:T(8,128)(2,1)} %copy.166), channel_id=1, source_target_pairs={{0,4},{4,0},{8,12},{12,8},{16,20},{20,16},{24,28},{28,24},{1,5},{5... | collective-permute-start | bytes 2985992 | tf_op jit(solution)/shard_map/ppermute | solution.py:27
  436.8 24.0 %collective-permute-start.31 = (bf16[256,1152]{0,1:T(8,128)(2,1)}, bf16[256,1152]{0,1:T(8,128)(2,1)S(1)}, u32[]{:S(2)}, u32[]{:S(2)}) collective-permute-start(bf16[256,1152]{0,1:T(8,128)(2,1)} %slice.506), channel_id=1, source_target_pairs={{0,2},{1,3},{2,0},{3,1},{4,6},{5,7},{6,4},{7,5},{8,10},{9,11},{10,... | collective-permute-start | bytes 1769480 | tf_op jit(solution)/shard_map/ppermute | solution.py:27
  442.6 23.7 %collective-permute-start.45 = (bf16[144,288]{0,1:T(8,128)(2,1)}, bf16[144,288]{0,1:T(8,128)(2,1)}, u32[]{:S(2)}, u32[]{:S(2)}) collective-permute-start(bf16[144,288]{0,1:T(8,128)(2,1)} %slice.513), channel_id=1, source_target_pairs={{0,16},{4,20},{8,24},{12,28},{16,0},{20,4},{24,8},{28,12},{1,17},{... | collective-permute-start | bytes 248840 | tf_op jit(solution)/shard_map/ppermute | solution.py:27
  480.1 23.4 %collective-permute-start.34 = (bf16[1,4,6,144]{3,1,2,0:T(4,128)(2,1)S(1)}, bf16[1,4,6,144]{3,1,2,0:T(4,128)(2,1)S(1)}, u32[]{:S(2)}, u32[]{:S(2)}) collective-permute-start(bf16[1,4,6,144]{3,1,2,0:T(4,128)(2,1)S(1)} %get-tuple-element.391), channel_id=1, source_target_pairs={{0,4},{4,0},{8,12},{12,8},{16,20},{20,16},{24,28},{28,24},{1,5},{5... | collective-permute-start | bytes 20744 | tf_op jit(solution)/shard_map/ppermute | solution.py:27
  512.7 32.8 %collective-permute-start.37 = (f32[4,288]{1,0:T(4,128)S(1)}, f32[4,288]{1,0:T(4,128)S(1)}, u32[]{:S(2)}, u32[]{:S(2)}) collective-permute-start(f32[4,288]{1,0:T(4,128)S(1)} %slice.342), channel_id=1, source_target_pairs={{0,4},{4,0},{8,12},{12,8},{16,20},{20,16},{24,28},{28,24},{1,5},{5... | collective-permute-start | bytes 13832 | tf_op jit(solution)/shard_map/ppermute | solution.py:27
  (145 other events, 1269.3 us)

commit v2 on v1

v2 whole, which is shorter than its diff:
```python
import jax
import jax.numpy as jnp
import numpy as np
from jax import lax
from jax.sharding import PartitionSpec as P

HEAD_DIM = 72
STEP = 10

EPS_NORM = 1e-06
CLIP_NORM = 1.0
LEARN_RATE = 0.05
WEIGHT_DECAY = 0.1
BETA_ONE = 0.9
BETA_TWO = 0.999
EPS_ADAM = 1e-08

LOW = jnp.bfloat16
WIDE = jnp.float32


def bit_count(size):
    return size.bit_length() - 1


def flip(value, axis, size, bit):
    return lax.ppermute(value, axis, [(i, i ^ (1 << bit)) for i in range(size)])


def grow(value, axis, size, bit):
    return jnp.concatenate([value, flip(value, axis, size, bit)], axis=0)


def shrink(value, axis, size, bit):
    half = value.shape[0] // 2
    moved = flip(value[half:].astype(LOW), axis, size, bit)
    return value[:half] + moved.astype(WIDE)


def gather_rel(value, axis, size):
    for bit in reversed(range(bit_count(size))):
        value = grow(value, axis, size, bit)
    return value


def scatter_rel(value, axis, size):
    for bit in range(bit_count(size)):
        value = shrink(value, axis, size, bit)
    return value


def spread_features(value, axis, size, bit):
    pairs = value.reshape((value.shape[0] // 2, 2) + value.shape[1:])
    moved = flip(pairs[:, 1], axis, size, bit)
    return jnp.concatenate([pairs[:, 0], moved], axis=-1)


def fold_features(value, axis, size):
    value = value[None]
    for bit in range(bit_count(size)):
        half = value.shape[-1] // 2
        moved = flip(value[..., half:], axis, size, bit)
        value = jnp.stack([value[..., :half], moved], axis=1)
        value = value.reshape((-1,) + value.shape[2:])
    return value


def sum_all(value, axis, size):
    for bit in range(bit_count(size)):
        value = value + flip(value, axis, size, bit)
    return value


def pin(*values):
    return lax.optimization_barrier(values)


def reversed_bits(size):
    bits = bit_count(size)
    return np.array([int(format(i, f"0{bits}b")[::-1], 2) if bits else 0 for i in range(size)])


def selection(index, size, width):
    block = width // size
    place = np.arange(width)
    source = (index ^ jnp.asarray(reversed_bits(size)[place // block], jnp.int32)) * block
    source = source + jnp.asarray(place % block, jnp.int32)
    return (lax.broadcasted_iota(jnp.int32, (width, width), 0) == source[None, :]).astype(LOW)


def matmul(left, right, dims):
    return lax.dot_general(left, right, (dims, ((), ())), preferred_element_type=WIDE)


def normalize(values):
    centre = values - jnp.mean(values, axis=-1, keepdims=True)
    spread = jnp.mean(centre * centre, axis=-1, keepdims=True)
    inverse = lax.rsqrt(spread + EPS_NORM)
    return centre * inverse, inverse


def normalize_back(normed, inverse, grad):
    mean_grad = jnp.mean(grad, axis=-1, keepdims=True)
    mean_both = jnp.mean(grad * normed, axis=-1, keepdims=True)
    return inverse * (grad - mean_grad - normed * mean_both)


def gelu_tanh(values):
    return jax.nn.gelu(values, approximate=True)


def attend(queries, key_rows, values):
    score_scale = HEAD_DIM ** (-0.5)
    scores = (
        jnp.einsum("qhe,khe->hqk", queries, key_rows, preferred_element_type=WIDE) * score_scale
    )
    row_peak = jnp.max(scores, axis=-1, keepdims=True)
    exponent = jnp.exp(scores - row_peak)
    row_total = jnp.sum(exponent, axis=-1, keepdims=True)
    probability = (exponent / row_total).astype(LOW)
    mixture = jnp.einsum("hqk,khe->qhe", probability, values, preferred_element_type=WIDE)
    return mixture.astype(LOW), row_peak + jnp.log(row_total)


def attend_back(queries, key_rows, values, log_total, grad_attended):
    score_scale = HEAD_DIM ** (-0.5)
    scores = (
        jnp.einsum("qhe,khe->hqk", queries, key_rows, preferred_element_type=WIDE) * score_scale
    )
    probability = jnp.exp(scores - log_total)
    grad_probability = jnp.einsum("qhe,khe->hqk", grad_attended, values, preferred_element_type=WIDE)
    row_inner = jnp.sum(probability * grad_probability, axis=-1, keepdims=True)
    grad_scores = (probability * (grad_probability - row_inner)).astype(LOW)
    grad_query = (
        jnp.einsum("hqk,khe->qhe", grad_scores, key_rows, preferred_element_type=WIDE) * score_scale
    )
    grad_keys = (
        jnp.einsum("hqk,qhe->khe", grad_scores, queries, preferred_element_type=WIDE) * score_scale
    )
    grad_values = jnp.einsum(
        "hqk,qhe->khe", probability.astype(LOW), grad_attended, preferred_element_type=WIDE
    )
    return grad_query.astype(LOW), grad_keys, grad_values


def adam_update(weight, gradient, moment, square, clip_factor):
    clipped = gradient * clip_factor
    moment_new = BETA_ONE * moment + (1.0 - BETA_ONE) * clipped
    square_new = BETA_TWO * square + (1.0 - BETA_TWO) * clipped * clipped
    mean_hat = moment_new / (1.0 - BETA_ONE**STEP)
    square_hat = square_new / (1.0 - BETA_TWO**STEP)
    weight_new = weight - LEARN_RATE * (
        mean_hat / (jnp.sqrt(square_hat) + EPS_ADAM) + WEIGHT_DECAY * weight
    )
    return (weight_new, moment_new, square_new)


def on_device(
    dp,
    tp,
    tokens,
    conditioning,
    out_grad,
    qkv_weight,
    out_weight,
    up_weight,
    down_weight,
    ada_weight,
    qkv_moment,
    out_moment,
    up_moment,
    down_moment,
    ada_moment,
    qkv_square,
    out_square,
    up_square,
    down_square,
    ada_square,
):
    width = tokens.shape[-1]
    heads_width = out_weight.shape[-1]
    here = lax.axis_index("dp")
    select = selection(here, dp, width)
    low_bits = bit_count(dp)
    high_bits = range(1, bit_count(tp))
    chunks = range(tp // 2)

    def swap(value, bit):
        return flip(value, "tensor", tp, bit)

    def widen(value):
        return jnp.concatenate([value, swap(value, 0)], axis=0)

    def all_blocks(value):
        pieces = [value]
        for bit in reversed(high_bits):
            pieces = pieces + [swap(piece, bit) for piece in pieces]
        return pieces

    def token_sum(kept, sent):
        part = [keep + swap(send, 0).astype(WIDE) for keep, send in zip(kept, sent)]
        for bit in high_bits:
            low_part = [value.astype(LOW) for value in part]
            moved = [swap(value, bit) for value in low_part]
            part = [
                low_part[k].astype(WIDE) + moved[k ^ (1 << (bit - 1))].astype(WIDE) for k in chunks
            ]
        return part

    def split_product(left, right, dims):
        rows = left.shape[0] // 2
        return pin(matmul(left[:rows], right, dims), matmul(left[rows:], right, dims).astype(LOW))

    signal, silu_back = jax.vjp(jax.nn.silu, conditioning)
    signal_all = gather_rel(signal.astype(LOW), "dp", dp)
    low_ada = ada_weight.astype(LOW)
    own_tokens = matmul(tokens[0], select, ((1,), (0,))).astype(LOW)
    own_grad = matmul(out_grad[0], select, ((1,), (0,))).astype(LOW)
    tokens_low = [widen(piece) for piece in all_blocks(own_tokens)]
    full_qkv = jnp.concatenate([qkv_weight[t].astype(LOW) for t in range(3)], axis=1)
    full_qkv = grow(full_qkv, "dp", dp, low_bits - 1)
    modulation = jnp.einsum("pi,kni->pkn", signal_all, low_ada, preferred_element_type=WIDE)
    modulation = sum_all(modulation, "tensor", tp)
    full_qkv, modulation = pin(full_qkv, modulation)
    full_up = out_weight.astype(LOW), up_weight.astype(LOW), down_weight.astype(LOW)
    full_out, full_up, full_down = (grow(w, "dp", dp, low_bits - 1) for w in full_up)
    for bit in reversed(range(1, low_bits)):
        modulation = spread_features(modulation, "dp", dp, bit)
    for bit in reversed(range(1, low_bits - 1)):
        full_qkv = grow(full_qkv, "dp", dp, bit)
    full_qkv, modulation, full_out, full_up = pin(full_qkv, modulation, full_out, full_up)
    modulation = spread_features(modulation, "dp", dp, 0)
    full_qkv = grow(full_qkv, "dp", dp, 0)
    for bit in reversed(range(1, low_bits - 1)):
        full_out = grow(full_out, "dp", dp, bit)
        full_up = grow(full_up, "dp", dp, bit)
    modulation = modulation.reshape(6, 1, width)
    shift_one, scale_one, gate_one, shift_two, scale_two, gate_two = modulation

    tokens_wide = [value.astype(WIDE) for value in tokens_low]
    norm_one, inverse_one = zip(*(pin(*normalize(value)) for value in tokens_wide))
    normed_one = [(value * (1.0 + scale_one) + shift_one).astype(LOW) for value in norm_one]
    normed_one = jnp.concatenate(normed_one, axis=0)
    normed_one, full_qkv, full_down = pin(normed_one, full_qkv, full_down)
    for bit in reversed(range(1, low_bits - 1)):
        full_down = grow(full_down, "dp", dp, bit)
    projected = matmul(normed_one, full_qkv, ((1,), (0,))).astype(LOW)
    projected, full_out, full_up = pin(projected, full_out, full_up)
    full_out = grow(full_out, "dp", dp, 0)
    full_up = grow(full_up, "dp", dp, 0)
    grad_low = [widen(piece) for piece in all_blocks(own_grad)]
    length = projected.shape[0]
    heads_split = projected.reshape(length, 3, heads_width // HEAD_DIM, HEAD_DIM)
    queries, key_rows, values = heads_split[:, 0], heads_split[:, 1], heads_split[:, 2]
    chunk_rows = length // len(chunks)
    query_parts = [queries[k * chunk_rows : (k + 1) * chunk_rows] for k in chunks]
    mixed, log_totals = zip(*(attend(part, key_rows, values) for part in query_parts))
    attended = [part.reshape(chunk_rows, heads_width) for part in mixed]
    attended[0], full_out, full_down = pin(attended[0], full_out, full_down)
    attn_terms = zip(*(split_product(part, full_out, ((1,), (1,))) for part in attended))
    attn_rows = token_sum(*attn_terms)
    own_rows = attn_rows[0].shape[0]
    middle = [tokens_wide[k][:own_rows] + gate_one * attn_rows[k] for k in chunks]
    norm_two, inverse_two = zip(*(normalize(value) for value in middle))
    normed_two = [(value * (1.0 + scale_two) + shift_two).astype(LOW) for value in norm_two]
    normed_two[0], full_up = pin(normed_two[0], full_up)
    full_down = grow(full_down, "dp", dp, 0)
    seq_two = [widen(value) for value in normed_two]

    pre_act = [matmul(part, full_up, ((1,), (0,))) for part in seq_two]
    activated, gelu_back = zip(*(jax.vjp(gelu_tanh, part) for part in pre_act))
    hidden = [part.astype(LOW) for part in activated]

    grad_mlp = [(part.astype(WIDE) * gate_two).astype(LOW) for part in grad_low]
    grad_hidden = [matmul(part, full_down, ((1,), (0,))) for part in grad_mlp]
    grad_pre = [back(part)[0].astype(LOW) for back, part in zip(gelu_back, grad_hidden)]
    grad_terms = zip(*(split_product(part, full_up, ((1,), (1,))) for part in grad_pre))
    grad_normed_two = token_sum(*grad_terms)
    all_hidden = jnp.concatenate(hidden, axis=0)
    grad_down = matmul(jnp.concatenate(grad_mlp, axis=0), all_hidden, ((0,), (0,)))
    summed_down = scatter_rel(grad_down, "dp", dp)
    all_seq_two = jnp.concatenate(seq_two, axis=0)
    grad_up = matmul(all_seq_two, jnp.concatenate(grad_pre, axis=0), ((0,), (0,)))
    summed_up = scatter_rel(grad_up, "dp", dp)

    mlp_kept, mlp_sent = zip(*(split_product(part, full_down, ((1,), (1,))) for part in hidden))
    mlp_part = [keep + swap(send, 0).astype(WIDE) for keep, send in zip(mlp_kept, mlp_sent)]
    for bit in high_bits:
        mlp_part = [
            mlp_part[2 * k] + swap(mlp_part[2 * k + 1].astype(LOW), bit).astype(WIDE)
            for k in range(len(mlp_part) // 2)
        ]
    mlp_rows = mlp_part[0]
    block_out = (middle[0] + gate_two * mlp_rows).astype(LOW)
    block_out = matmul(block_out, select, ((1,), (1,))).astype(LOW)
    grad_gate_two = jnp.sum(own_grad.astype(WIDE) * mlp_rows, axis=0)

    grad_shift_two = jnp.sum(grad_normed_two[0], axis=0)
    grad_scale_two = jnp.sum(grad_normed_two[0] * norm_two[0], axis=0)
    grad_middle = [
        grad_low[k][:own_rows].astype(WIDE)
        + normalize_back(norm_two[k], inverse_two[k], grad_normed_two[k] * (1.0 + scale_two))
        for k in chunks
    ]
    grad_gate_one = jnp.sum(grad_middle[0] * attn_rows[0], axis=0)

    grad_attn = [widen((part * gate_one).astype(LOW)) for part in grad_middle]
    grad_attended = [
        matmul(part, full_out, ((1,), (0,))).astype(LOW).reshape(queries[:chunk_rows].shape)
        for part in grad_attn
    ]
    grad_out = matmul(
        jnp.concatenate(grad_attn, axis=0), jnp.concatenate(attended, axis=0), ((0,), (0,))
    )
    summed_out = scatter_rel(grad_out, "dp", dp)
    parts = [
        attend_back(query_parts[k], key_rows, values, log_totals[k], grad_attended[k])
        for k in chunks
    ]
    grad_queries = jnp.concatenate([part[0] for part in parts], axis=0)
    grad_keys = sum(part[1] for part in parts).astype(LOW)
    grad_values = sum(part[2] for part in parts).astype(LOW)
    grad_projected = jnp.concatenate(
        [part.reshape(length, heads_width) for part in (grad_queries, grad_keys, grad_values)],
        axis=1,
    )
    grad_qkv = matmul(normed_one, grad_projected, ((0,), (0,)))
    grad_qkv, grad_projected = pin(grad_qkv, grad_projected)
    grad_qkv = shrink(grad_qkv, "dp", dp, 0)
    one_terms = [
        matmul(grad_projected[k * chunk_rows : (k + 1) * chunk_rows], full_qkv, ((1,), (1,)))
        for k in chunks
    ]

    grad_mod = jnp.stack(
        [
            sum(jnp.sum(one_terms[k], axis=0) for k in chunks),
            sum(jnp.sum(one_terms[k] * norm_one[k], axis=0) for k in chunks),
            grad_gate_one,
            grad_shift_two,
            grad_scale_two,
            grad_gate_two,
        ]
    )
    grad_mod = sum_all(grad_mod, "tensor", tp).astype(LOW)
    grad_mod, grad_qkv = pin(grad_mod, grad_qkv)
    for bit in range(1, low_bits):
        grad_qkv = shrink(grad_qkv, "dp", dp, bit)
    summed_qkv = jnp.stack(
        [grad_qkv[:, t * heads_width : (t + 1) * heads_width] for t in range(3)], axis=0
    )
    grad_mod = fold_features(grad_mod, "dp", dp)
    summed_ada = jnp.einsum("pkn,pi->kni", grad_mod, signal_all, preferred_element_type=WIDE)
    total = jnp.sum(summed_out * summed_out) + jnp.sum(summed_ada * summed_ada)
    total = total + jnp.sum(summed_up * summed_up) + jnp.sum(summed_down * summed_down)
    total = total + jnp.sum(grad_qkv * grad_qkv)

    one_part = [
        terms[:own_rows] + swap(terms[own_rows:].astype(LOW), 0).astype(WIDE) for terms in one_terms
    ]
    for bit in high_bits:
        one_part = [
            one_part[2 * k] + swap(one_part[2 * k + 1].astype(LOW), bit).astype(WIDE)
            for k in range(len(one_part) // 2)
        ]
    input_grad = grad_middle[0] + normalize_back(
        norm_one[0][:own_rows], inverse_one[0][:own_rows], one_part[0] * (1.0 + scale_one)
    )
    coarse = input_grad.astype(LOW)
    fine = (input_grad - coarse.astype(WIDE)).astype(LOW)
    input_grad = matmul(coarse, select, ((1,), (1,))) + matmul(fine, select, ((1,), (1,)))
    grad_signal = jnp.einsum("pkn,kni->pi", grad_mod, low_ada, preferred_element_type=WIDE)
    for bit in range(low_bits):
        part = grad_signal.shape[0] // 2
        grad_signal = grad_signal[:part] + flip(grad_signal[part:], "dp", dp, bit)
    cond_grad = silu_back(grad_signal)[0]

    total = sum_all(sum_all(total, "tensor", tp), "dp", dp)
    grad_norm = jnp.sqrt(total)
    clip_factor = CLIP_NORM / jnp.maximum(grad_norm, CLIP_NORM)
    qkv = adam_update(qkv_weight, summed_qkv, qkv_moment, qkv_square, clip_factor)
    out = adam_update(out_weight, summed_out, out_moment, out_square, clip_factor)
    up = adam_update(up_weight, summed_up, up_moment, up_square, clip_factor)
    down = adam_update(down_weight, summed_down, down_moment, down_square, clip_factor)
    ada = adam_update(ada_weight, summed_ada, ada_moment, ada_square, clip_factor)
    return (
        block_out[None],
        input_grad[None],
        cond_grad,
        grad_norm,
        *(new for group in zip(qkv, out, up, down, ada) for new in group),
    )


def solution(mesh):
    dp, tp = mesh.shape["dp"], mesh.shape["tensor"]
    rows = P("dp", "tensor", None)
    plain = P("dp", "tensor")
    stacked = P(None, "dp", "tensor")
    weights = (stacked, plain, plain, plain, stacked)

    def step(*arrays):
        return on_device(dp, tp, *arrays)

    return jax.shard_map(
        step,
        mesh=mesh,
        in_specs=(rows, plain, rows) + weights * 3,
        out_specs=(rows, rows, plain, P()) + weights * 3,
        check_vma=False,
    )
```

time: 564 us -> 498 us (0.88)
  local copies, waits for them, and re-layouts: 97.9 us -> 49.3 us
  other arithmetic: 99.5 us -> 65.5 us
  matrix products: 91 us -> 112 us
  waiting for transfers between devices: 194 us -> 175 us
  starting transfers between devices: 63.7 us -> 81.5 us
    rev x2 -> x0, local copies, waits for them, and re-layouts: 21.8 us -> none  [sum_half(): moved = blocks[:, ::-1].reshape(moved.shape)]
    ppermute x57 -> x69, waiting for transfers between devices: 194 us -> 175 us  [flip(): return lax.ppermute(value, axis, [(i, i ^ 1 << bit) for i in range(size)])]
    ppermute x57 -> x69, starting transfers between devices: 63.7 us -> 81.5 us  [flip(): return lax.ppermute(value, axis, [(i, i ^ 1 << bit) for i in range(size)])]
    dot_general x17 -> x30, matrix products: 63.3 us -> 80.7 us  [matmul(): lax.dot_general(left, right, (dims, ((), ())), preferred_element_type=WIDE)]
    concatenate x13 -> x19, other arithmetic: 21.1 us -> 6.19 us  [the longest x13 5.43 us: grow(): return jnp.concatenate([value, flip(value, axis, size, bit)], axis=0)]
    another operation x23 -> x11, local copies, waits for them, and re-layouts: 9.84 us -> 1.29 us  [the longest x1 0.95 us: on_device(): jnp.stack([grad_qkv[:, t * heads_width:(t + 1) * heads_width] for t in ra...]
    reshape x4 -> x3, local copies, waits for them, and re-layouts: 7.78 us -> 0.09 us  [the longest x2 0.06 us: fold_features(): value = value.reshape((-1,) + value.shape[2:])]
    reduce_sum x8 -> x6, other arithmetic: 17.5 us -> 10.3 us  [the longest x2 3.72 us: attend(): row_total = jnp.sum(exponent, axis=-1, keepdims=True)]
  transfers between devices with their start and end apart: 57 -> 69, of which waited for: 26 -> 29; matrix products, arithmetic and copies ran while one was open for 40% -> 34% of each run, Pallas kernels for 0% -> 0%
where the time goes in v2:
time: 498 us; the launch traced here: 494 us
  waiting for transfers between devices  175 us (35%)
  matrix products  112 us (22%)
  starting transfers between devices  81.5 us (16%)
  other arithmetic  65.5 us (13%)
  local copies, waits for them, and re-layouts  49.3 us (10%)
  between operations  10.1 us (2%)
    ppermute x69, waiting for transfers between devices, flip(): return lax.ppermute(value, axis, [(i, i ^ 1 << bit) for i in range(size)])  175 us
    ppermute x69, starting transfers between devices, flip(): return lax.ppermute(value, axis, [(i, i ^ 1 << bit) for i in range(size)])  81.5 us
    dot_general x30, matrix products, matmul(): lax.dot_general(left, right, (dims, ((), ())), preferred_element_type=WIDE)  80.7 us
    unnamed x206, local copies, waits for them, and re-layouts  20.7 us
    slice x13, local copies, waits for them, and re-layouts, shrink(): moved = flip(value[half:].astype(LOW), axis, size, bit)  14.2 us
    sub x5, other arithmetic, adam_update(): weight - LEARN_RATE * (mean_hat / (jnp.sqrt(square_hat) + EPS_ADAM) + WEI...  11.5 us
  transfers between devices with their start and end apart: 69, of which 29 were waited for; matrix products, arithmetic and copies ran while one was open for 34% of the time, Pallas kernels for 0%

profile of v2, /device:TPU:0, one launch (start us, length us, event | category | flops | bytes accessed | tf_op | source)
XLA Modules:
  0.0 493.8 jit_solution(4888537411133222935)
XLA Ops:
  38.1 7.7 %collective-permute-done.8 = f32[4,6,144]{2,0,1:T(4,128)} collective-permute-done((f32[4,6,144]{2,0,1:T(4,128)}, f32[4,6,144]{2,0,1:T(4,128)}, u32[]{:S(2)}, u32[]{:S(2)}) %collective-permute-start.8) | collective-permute-done | bytes 13856 | tf_op jit(solution)/shard_map/ppermute | solution.py:27
  46.8 4.5 collective-permute-start.9
  56.1 7.1 %collective-permute-done.16 = bf16[144,1152]{1,0:T(8,128)(2,1)} collective-permute-done((bf16[144,1152]{1,0:T(8,128)(2,1)}, bf16[144,1152]{1,0:T(8,128)(2,1)}, u32[]{:S(2)}, u32[]{:S(2)}) %collective-permute-start.16) | collective-permute-done | bytes 331808 | tf_op jit(solution)/shard_map/ppermute | solution.py:27
  65.4 10.4 %collective-permute-done.7 = bf16[288,864]{1,0:T(8,128)(2,1)S(1)} collective-permute-done((bf16[288,864]{1,0:T(8,128)(2,1)S(1)}, bf16[288,864]{1,0:T(8,128)(2,1)S(1)}, u32[]{:S(2)}, u32[]{:S(2)}) %collective-permute-start.7) | collective-permute-done | bytes 497696 | tf_op jit(solution)/shard_map/ppermute | solution.py:27
  87.4 9.0 %collective-permute-done.18 = bf16[288,1152]{1,0:T(8,128)(2,1)S(1)} collective-permute-done((bf16[288,1152]{1,0:T(8,128)(2,1)S(1)}, bf16[288,1152]{1,0:T(8,128)(2,1)S(1)}, u32[]{:S(2)}, u32[]{:S(2)}) %collective-permute-start.18) | collective-permute-done | bytes 663584 | tf_op jit(solution)/shard_map/ppermute | solution.py:27
  96.5 6.0 %collective-permute-done.15 = bf16[576,864]{1,0:T(8,128)(2,1)S(1)} collective-permute-done((bf16[576,864]{1,0:T(8,128)(2,1)S(1)}, bf16[576,864]{1,0:T(8,128)(2,1)S(1)}, u32[]{:S(2)}, u32[]{:S(2)}) %collective-permute-start.15) | collective-permute-done | bytes 995360 | tf_op jit(solution)/shard_map/ppermute | solution.py:27
  120.8 9.2 %collective-permute-done.19 = bf16[576,288]{1,0:T(8,128)(2,1)S(1)} collective-permute-done((bf16[576,288]{1,0:T(8,128)(2,1)S(1)}, bf16[576,288]{1,0:T(8,128)(2,1)S(1)}, u32[]{:S(2)}, u32[]{:S(2)}) %collective-permute-start.19) | collective-permute-done | bytes 331808 | tf_op jit(solution)/shard_map/ppermute | solution.py:27
  130.1 4.6 collective-permute-done.20
  141.0 17.6 %collective-permute-done.24 = bf16[576,1152]{1,0:T(8,128)(2,1)} collective-permute-done((bf16[576,1152]{1,0:T(8,128)(2,1)S(1)}, bf16[576,1152]{1,0:T(8,128)(2,1)}, u32[]{:S(2)}, u32[]{:S(2)}) %collective-permute-start.24) | collective-permute-done | bytes 1327136 | tf_op jit(solution)/shard_map/ppermute | solution.py:27
  162.4 21.9 %collective-permute-done.26 = bf16[576,1152]{1,0:T(8,128)(2,1)S(1)} collective-permute-done((bf16[576,1152]{1,0:T(8,128)(2,1)S(1)}, bf16[576,1152]{1,0:T(8,128)(2,1)S(1)}, u32[]{:S(2)}, u32[]{:S(2)}) %collective-permute-start.26) | collective-permute-done | bytes 1327136 | tf_op jit(solution)/shard_map/ppermute | solution.py:27
  192.2 16.6 %fusion.45 = (bf16[512,1152]{1,0:T(8,128)(2,1)S(1)}, bf16[512,1152]{1,0:T(8,128)(2,1)S(1)}) fusion(f32[512,1152]{1,0:T(8,128)} %fusion.183, bf16[1152,1152]{1,0:T(8,128)(2,1)S(1)} %pad_maximum_fusion, bf16[256,1152]{1,0:T(8,128)(2,1)S(1)} %collective-permute-done.29, bf16[256,1152]{1,0:T(8,128)(2,1)S(1)} %get-tuple-element.255), kind=kOutput, calls=%fused_computation.71 | convolution fusion | flops 1374289920 | bytes 8552448 | tf_op jit(solution)/shard_map/dot_general | solution.py:92
  220.7 4.6 fusion.65
  226.0 6.0 %convolution_convert_fusion.2 = bf16[256,1152]{1,0:T(8,128)(2,1)} fusion(bf16[1152,1152]{1,0:T(8,128)(2,1)} %copy-done.59, bf16[512,1152]{1,0:T(8,128)(2,1)} %copy-done.94), kind=kOutput, calls=%fused_computation.48 | convolution fusion | flops 679772160 | bytes 3833856 | tf_op jit(solution)/shard_map/dot_general | solution.py:92
  236.8 5.7 %fusion.54 = f32[1152,1152]{1,0:T(8,128)S(1)} fusion(bf16[256,1152]{1,0:T(8,128)(2,1)} %copy-done.90, bf16[256,1152]{1,0:T(8,128)(2,1)} %copy-done.65, bf16[256,1152]{1,0:T(8,128)(2,1)} %copy-done.91, bf16[256,1152]{1,0:T(8,128)(2,1)} %copy-done.66, bf16[512,1152]{1,0:T(8,128)(2,1)} %copy-done.92, bf16[512,1152]{1,0:T(8,128)(2,1)} %copy-done.93), kind=kOutput, calls=%fused_computation.81 | convolution fusion | flops 2732064768 | bytes 10027008 | tf_op jit(solution)/shard_map/dot_general | solution.py:92
  252.3 11.1 %collective-permute-done.39 = bf16[256,1152]{1,0:T(8,128)(2,1)} collective-permute-done((bf16[256,1152]{1,0:T(8,128)(2,1)S(1)}, bf16[256,1152]{1,0:T(8,128)(2,1)}, u32[]{:S(2)}, u32[]{:S(2)}) %collective-permute-start.39) | collective-permute-done | bytes 589856 | tf_op jit(solution)/shard_map/ppermute | solution.py:27
  266.2 9.3 %collective-permute-done.31 = bf16[256,1152]{1,0:T(8,128)(2,1)S(1)} collective-permute-done((bf16[256,1152]{1,0:T(8,128)(2,1)S(1)}, bf16[256,1152]{1,0:T(8,128)(2,1)S(1)}, u32[]{:S(2)}, u32[]{:S(2)}) %collective-permute-start.31) | collective-permute-done | bytes 589856 | tf_op jit(solution)/shard_map/ppermute | solution.py:27
  295.3 4.7 multiply_reduce_fusion.1
  300.0 4.5 multiply_convert_fusion.1
  318.3 4.4 fusion.170
  342.3 5.6 %copy.123 = f32[1152,864]{1,0:T(8,128)} copy(f32[1152,864]{0,1:T(8,128)} %fusion.170) | data formatting | bytes 7962624 | tf_op jit(solution)/shard_map/optimization_barrier | solution.py:75
  363.6 24.2 %collective-permute-done.53 = bf16[576,288]{0,1:T(8,128)(2,1)S(1)} collective-permute-done((bf16[576,288]{0,1:T(8,128)(2,1)S(1)}, bf16[576,288]{0,1:T(8,128)(2,1)S(1)}, u32[]{:S(2)}, u32[]{:S(2)}) %collective-permute-start.53) | collective-permute-done | bytes 331808 | tf_op jit(solution)/shard_map/ppermute | solution.py:27
  392.7 9.0 %collective-permute-done.54 = bf16[288,288]{0,1:T(8,128)(2,1)S(1)} collective-permute-done((bf16[288,288]{0,1:T(8,128)(2,1)S(1)}, bf16[288,288]{0,1:T(8,128)(2,1)S(1)}, u32[]{:S(2)}, u32[]{:S(2)}) %collective-permute-start.54) | collective-permute-done | bytes 165920 | tf_op jit(solution)/shard_map/ppermute | solution.py:27
  446.3 4.8 collective-permute-done.63
  480.9 4.5 multiply_subtract_fusion
  (507 shorter events, 270.9 us)
Async XLA Ops:
  20.5 43.7 %collective-permute-start = (bf16[256,1152]{1,0:T(8,128)(2,1)S(1)}, bf16[256,1152]{1,0:T(8,128)(2,1)S(1)}, u32[]{:S(2)}, u32[]{:S(2)}) collective-permute-start(bf16[256,1152]{1,0:T(8,128)(2,1)S(1)} %fusion.31), channel_id=1, source_target_pairs={{0,1},{1,0},{2,3},{3,2},{4,5},{5,4},{6,7},{7,6},{8,9},{9,8},{10,11... | collective-permute-start | bytes 1769480 | tf_op jit(solution)/shard_map/ppermute | solution.py:27
  20.6 44.3 %collective-permute-start.13 = (bf16[256,1152]{1,0:T(8,128)(2,1)S(1)}, bf16[256,1152]{1,0:T(8,128)(2,1)S(1)}, u32[]{:S(2)}, u32[]{:S(2)}) collective-permute-start(bf16[256,1152]{1,0:T(8,128)(2,1)S(1)} %fusion.31), channel_id=1, source_target_pairs={{0,2},{1,3},{2,0},{3,1},{4,6},{5,7},{6,4},{7,5},{8,10},{9,11},{10,... | collective-permute-start | bytes 1769480 | tf_op jit(solution)/shard_map/ppermute | solution.py:27
  21.8 24.9 %collective-permute-start.10 = (bf16[144,288]{1,0:T(8,128)(2,1)}, bf16[144,288]{1,0:T(8,128)(2,1)}, u32[]{:S(2)}, u32[]{:S(2)}) collective-permute-start(bf16[144,288]{1,0:T(8,128)(2,1)} %convert_element_type.324), channel_id=1, source_target_pairs={{0,16},{4,20},{8,24},{12,28},{16,0},{20,4},{24,8},{28,12},{1,17},{... | collective-permute-start | bytes 248840 | tf_op jit(solution)/shard_map/ppermute | solution.py:27
  24.5 28.9 %collective-permute-start.11 = (bf16[144,1152]{1,0:T(8,128)(2,1)}, bf16[144,1152]{1,0:T(8,128)(2,1)}, u32[]{:S(2)}, u32[]{:S(2)}) collective-permute-start(bf16[144,1152]{1,0:T(8,128)(2,1)} %convert_element_type.325), channel_id=1, source_target_pairs={{0,16},{4,20},{8,24},{12,28},{16,0},{20,4},{24,8},{28,12},{1,17},{... | collective-permute-start | bytes 995336 | tf_op jit(solution)/shard_map/ppermute | solution.py:27
  53.3 32.1 %collective-permute-start.32 = (bf16[256,1152]{1,0:T(8,128)(2,1)S(1)}, bf16[256,1152]{1,0:T(8,128)(2,1)S(1)}, u32[]{:S(2)}, u32[]{:S(2)}) collective-permute-start(bf16[256,1152]{1,0:T(8,128)(2,1)S(1)} %fusion.29), channel_id=1, source_target_pairs={{0,1},{1,0},{2,3},{3,2},{4,5},{5,4},{6,7},{7,6},{8,9},{9,8},{10,11... | collective-permute-start | bytes 1769480 | tf_op jit(solution)/shard_map/ppermute | solution.py:27
  53.4 23.9 %collective-permute-start.34 = (bf16[256,1152]{1,0:T(8,128)(2,1)S(1)}, bf16[256,1152]{1,0:T(8,128)(2,1)S(1)}, u32[]{:S(2)}, u32[]{:S(2)}) collective-permute-start(bf16[256,1152]{1,0:T(8,128)(2,1)S(1)} %fusion.29), channel_id=1, source_target_pairs={{0,2},{1,3},{2,0},{3,1},{4,6},{5,7},{6,4},{7,5},{8,10},{9,11},{10,... | collective-permute-start | bytes 1769480 | tf_op jit(solution)/shard_map/ppermute | solution.py:27
  79.6 22.9 %collective-permute-start.15 = (bf16[576,864]{1,0:T(8,128)(2,1)S(1)}, bf16[576,864]{1,0:T(8,128)(2,1)S(1)}, u32[]{:S(2)}, u32[]{:S(2)}) collective-permute-start(bf16[576,864]{1,0:T(8,128)(2,1)S(1)} %pad_maximum_fusion.8), channel_id=1, source_target_pairs={{0,4},{4,0},{8,12},{12,8},{16,20},{20,16},{24,28},{28,24},{1,5},{5... | collective-permute-start | bytes 2985992 | tf_op jit(solution)/shard_map/ppermute | solution.py:27
  120.3 38.2 %collective-permute-start.24 = (bf16[576,1152]{1,0:T(8,128)(2,1)S(1)}, bf16[576,1152]{1,0:T(8,128)(2,1)}, u32[]{:S(2)}, u32[]{:S(2)}) collective-permute-start(bf16[576,1152]{1,0:T(8,128)(2,1)S(1)} %pad_maximum_fusion.4), channel_id=1, source_target_pairs={{0,4},{4,0},{8,12},{12,8},{16,20},{20,16},{24,28},{28,24},{1,5},{5... | collective-permute-start | bytes 3981320 | tf_op jit(solution)/shard_map/ppermute | solution.py:27
  137.2 22.9 %collective-permute-start.22 = (bf16[256,1152]{1,0:T(8,128)(2,1)S(1)}, bf16[256,1152]{1,0:T(8,128)(2,1)S(1)}, u32[]{:S(2)}, u32[]{:S(2)}) collective-permute-start(bf16[256,1152]{1,0:T(8,128)(2,1)S(1)} %convolution_convert_fusion.4), channel_id=1, source_target_pairs={{0,1},{1,0},{2,3},{3,2},{4,5},{5,4},{6,7},{7,6},{8,9},{9,8},{10,11... | collective-permute-start | bytes 1769480 | tf_op jit(solution)/shard_map/ppermute | solution.py:27
  137.7 46.6 %collective-permute-start.26 = (bf16[576,1152]{1,0:T(8,128)(2,1)S(1)}, bf16[576,1152]{1,0:T(8,128)(2,1)S(1)}, u32[]{:S(2)}, u32[]{:S(2)}) collective-permute-start(bf16[576,1152]{1,0:T(8,128)(2,1)S(1)} %pad_maximum_fusion.5), channel_id=1, source_target_pairs={{0,4},{4,0},{8,12},{12,8},{16,20},{20,16},{24,28},{28,24},{1,5},{5... | collective-permute-start | bytes 3981320 | tf_op jit(solution)/shard_map/ppermute | solution.py:27
  160.6 24.0 %collective-permute-start.23 = (bf16[256,1152]{1,0:T(8,128)(2,1)S(1)}, bf16[256,1152]{1,0:T(8,128)(2,1)S(1)}, u32[]{:S(2)}, u32[]{:S(2)}) collective-permute-start(bf16[256,1152]{1,0:T(8,128)(2,1)S(1)} %get-tuple-element.225), channel_id=1, source_target_pairs={{0,2},{1,3},{2,0},{3,1},{4,6},{5,7},{6,4},{7,5},{8,10},{9,11},{10,... | collective-permute-start | bytes 1769480 | tf_op jit(solution)/shard_map/ppermute | solution.py:27
  234.3 31.9 %collective-permute-start.27 = (bf16[256,1152]{1,0:T(8,128)(2,1)}, bf16[256,1152]{1,0:T(8,128)(2,1)}, u32[]{:S(2)}, u32[]{:S(2)}) collective-permute-start(bf16[256,1152]{1,0:T(8,128)(2,1)} %convolution_convert_fusion.3), channel_id=1, source_target_pairs={{0,1},{1,0},{2,3},{3,2},{4,5},{5,4},{6,7},{7,6},{8,9},{9,8},{10,11... | collective-permute-start | bytes 1769480 | tf_op jit(solution)/shard_map/ppermute | solution.py:27
  236.2 27.2 %collective-permute-start.39 = (bf16[256,1152]{1,0:T(8,128)(2,1)S(1)}, bf16[256,1152]{1,0:T(8,128)(2,1)}, u32[]{:S(2)}, u32[]{:S(2)}) collective-permute-start(bf16[256,1152]{1,0:T(8,128)(2,1)S(1)} %add_convert_fusion.3), channel_id=1, source_target_pairs={{0,2},{1,3},{2,0},{3,1},{4,6},{5,7},{6,4},{7,5},{8,10},{9,11},{10,... | collective-permute-start | bytes 1769480 | tf_op jit(solution)/shard_map/ppermute | solution.py:27
  243.7 40.5 %collective-permute-start.56 = (bf16[576,1152]{1,0:T(8,128)(2,1)}, bf16[576,1152]{1,0:T(8,128)(2,1)S(1)}, u32[]{:S(2)}, u32[]{:S(2)}) collective-permute-start(bf16[576,1152]{1,0:T(8,128)(2,1)} %slice.525), channel_id=1, source_target_pairs={{0,4},{4,0},{8,12},{12,8},{16,20},{20,16},{24,28},{28,24},{1,5},{5... | collective-permute-start | bytes 3981320 | tf_op jit(solution)/shard_map/ppermute | solution.py:27
  246.5 82.4 %collective-permute-start.59 = (bf16[576,1152]{1,0:T(8,128)(2,1)}, bf16[576,1152]{1,0:T(8,128)(2,1)}, u32[]{:S(2)}, u32[]{:S(2)}) collective-permute-start(bf16[576,1152]{1,0:T(8,128)(2,1)} %slice.524), channel_id=1, source_target_pairs={{0,4},{4,0},{8,12},{12,8},{16,20},{20,16},{24,28},{28,24},{1,5},{5... | collective-permute-start | bytes 3981320 | tf_op jit(solution)/shard_map/ppermute | solution.py:27
  250.8 24.7 %collective-permute-start.31 = (bf16[256,1152]{1,0:T(8,128)(2,1)S(1)}, bf16[256,1152]{1,0:T(8,128)(2,1)S(1)}, u32[]{:S(2)}, u32[]{:S(2)}) collective-permute-start(bf16[256,1152]{1,0:T(8,128)(2,1)S(1)} %add_convert_fusion.5), channel_id=1, source_target_pairs={{0,2},{1,3},{2,0},{3,1},{4,6},{5,7},{6,4},{7,5},{8,10},{9,11},{10,... | collective-permute-start | bytes 1769480 | tf_op jit(solution)/shard_map/ppermute | solution.py:27
  285.5 71.1 %collective-permute-start.57 = (bf16[288,1152]{1,0:T(8,128)(2,1)}, bf16[288,1152]{1,0:T(8,128)(2,1)}, u32[]{:S(2)}, u32[]{:S(2)}) collective-permute-start(bf16[288,1152]{1,0:T(8,128)(2,1)} %slice.528), channel_id=1, source_target_pairs={{0,8},{4,12},{8,0},{12,4},{16,24},{20,28},{24,16},{28,20},{1,9},{5... | collective-permute-start | bytes 1990664 | tf_op jit(solution)/shard_map/ppermute | solution.py:27
  333.7 24.9 %collective-permute-start.60 = (bf16[288,1152]{1,0:T(8,128)(2,1)}, bf16[288,1152]{1,0:T(8,128)(2,1)}, u32[]{:S(2)}, u32[]{:S(2)}) collective-permute-start(bf16[288,1152]{1,0:T(8,128)(2,1)} %slice.527), channel_id=1, source_target_pairs={{0,8},{4,12},{8,0},{12,4},{16,24},{20,28},{24,16},{28,20},{1,9},{5... | collective-permute-start | bytes 1990664 | tf_op jit(solution)/shard_map/ppermute | solution.py:27
  336.0 87.5 %collective-permute-start.42 = (bf16[256,1152]{1,0:T(8,128)(2,1)}, bf16[256,1152]{1,0:T(8,128)(2,1)}, u32[]{:S(2)}, u32[]{:S(2)}) collective-permute-start(bf16[256,1152]{1,0:T(8,128)(2,1)} %slice.529), channel_id=1, source_target_pairs={{0,1},{1,0},{2,3},{3,2},{4,5},{5,4},{6,7},{7,6},{8,9},{9,8},{10,11... | collective-permute-start | bytes 1769480 | tf_op jit(solution)/shard_map/ppermute | solution.py:27
  338.7 98.0 %collective-permute-start.41 = (bf16[256,1152]{1,0:T(8,128)(2,1)}, bf16[256,1152]{1,0:T(8,128)(2,1)}, u32[]{:S(2)}, u32[]{:S(2)}) collective-permute-start(bf16[256,1152]{1,0:T(8,128)(2,1)} %slice.530), channel_id=1, source_target_pairs={{0,1},{1,0},{2,3},{3,2},{4,5},{5,4},{6,7},{7,6},{8,9},{9,8},{10,11... | collective-permute-start | bytes 1769480 | tf_op jit(solution)/shard_map/ppermute | solution.py:27
  354.8 35.8 %collective-permute-start.46 = (bf16[576,864]{1,0:T(8,128)(2,1)}, bf16[576,864]{1,0:T(8,128)(2,1)S(1)}, u32[]{:S(2)}, u32[]{:S(2)}) collective-permute-start(bf16[576,864]{1,0:T(8,128)(2,1)} %copy.124), channel_id=1, source_target_pairs={{0,4},{4,0},{8,12},{12,8},{16,20},{20,16},{24,28},{28,24},{1,5},{5... | collective-permute-start | bytes 2985992 | tf_op jit(solution)/shard_map/ppermute | solution.py:27
  356.6 31.3 %collective-permute-start.53 = (bf16[576,288]{0,1:T(8,128)(2,1)S(1)}, bf16[576,288]{0,1:T(8,128)(2,1)S(1)}, u32[]{:S(2)}, u32[]{:S(2)}) collective-permute-start(bf16[576,288]{0,1:T(8,128)(2,1)S(1)} %slice.532), channel_id=1, source_target_pairs={{0,4},{4,0},{8,12},{12,8},{16,20},{20,16},{24,28},{28,24},{1,5},{5... | collective-permute-start | bytes 995336 | tf_op jit(solution)/shard_map/ppermute | solution.py:27
  358.6 49.2 %collective-permute-start.58 = (bf16[144,1152]{1,0:T(8,128)(2,1)S(1)}, bf16[144,1152]{1,0:T(8,128)(2,1)S(1)}, u32[]{:S(2)}, u32[]{:S(2)}) collective-permute-start(bf16[144,1152]{1,0:T(8,128)(2,1)S(1)} %slice.534), channel_id=1, source_target_pairs={{0,16},{4,20},{8,24},{12,28},{16,0},{20,4},{24,8},{28,12},{1,17},{... | collective-permute-start | bytes 995336 | tf_op jit(solution)/shard_map/ppermute | solution.py:27
  387.9 26.4 %collective-permute-start.61 = (bf16[144,1152]{1,0:T(8,128)(2,1)}, bf16[144,1152]{1,0:T(8,128)(2,1)S(1)}, u32[]{:S(2)}, u32[]{:S(2)}) collective-permute-start(bf16[144,1152]{1,0:T(8,128)(2,1)} %slice.533), channel_id=1, source_target_pairs={{0,16},{4,20},{8,24},{12,28},{16,0},{20,4},{24,8},{28,12},{1,17},{... | collective-permute-start | bytes 995336 | tf_op jit(solution)/shard_map/ppermute | solution.py:27
  (143 other events, 1547.6 us)
